TPU v7x, 256 devices: a whole 4x4x8 slice. The times are simulated.
256 devices in a mesh: gx: 8 (over z_lo, x), gy: 32 (over z_hi, y, core).
Axes of the slice: x: 4, y: 4, z: 8 (z_hi: 4, z_lo: 2; z = z_hi * 2 + z_lo), core: 2. Of those that a mesh axis runs over, the one named last changes fastest.
Arguments:
- velocity: float32 [3, 32, 128, 4096], P(None, None, 'gx', 'gy'), may hold values from -6 to 6
- viscosity: float32 [32, 128, 4096], P(None, 'gx', 'gy'), may hold values from 0.02 to 0.12
- marker_cells: int32 [8192, 3, 128], P(('gx', 'gy')), may hold values from 0 to 4095, as said below
- marker_offset: float32 [8192, 3, 128], P(('gx', 'gy')), may hold values from 0 to 1
- marker_force: float32 [8192, 3, 128], P(('gx', 'gy')), may hold values from -24 to 24
Outputs:
- fluid_velocity: float32 [3, 32, 128, 4096], P(None, None, 'gx', 'gy')
- marker_velocity: float32 [8192, 3, 128], P(('gx', 'gy'))
Inputs may be any that keep to these rules, and one draw needn't show every extreme that they name: `marker_cells`: within one block every marker's x lies in [i * 16, (i + 1) * 16) where i is the gx index of the device holding the block, every marker's y lies in one range [j * 128, (j + 1) * 128), and z lies in [1, 29]. One device holds at most 2 blocks whose y range is one given j, and in every gx column some j receives exactly 2 blocks from every device of that column.
All inputs are finite; a program needn't handle non-finite values.
Results may differ from a plain program's by a relative error of at most 0.0003.
The roundings to bfloat16 on the way count: a program that leaves them out, or rounds other values in their place, can miss the bound.
Values may be sent and summed in bfloat16 or wider, within the bound.
A program may use at most 128 MiB of HBM per device.

v0:
```python
import jax
import jax.numpy as jnp
from jax import lax
from jax.sharding import PartitionSpec as P

CAP = 2


OFFSETS = (-1, 0, 1, 2)
group_slots = 4


def padded_2(array, sides, width):
    for axis, dim in sides:
        count, length = (lax.axis_size(axis), array.shape[dim])
        up = [(i, (i + 1) % count) for i in range(count)]
        down = [(j, i) for i, j in up]
        last = lax.slice_in_dim(array, length - width, length, axis=dim)
        first = lax.slice_in_dim(array, 0, width, axis=dim)
        before = lax.ppermute(last, axis, up)
        after = lax.ppermute(first, axis, down)
        array = jnp.concatenate([before, array, after], axis=dim)
    return array


def peskin_weight(distance):
    magnitude = jnp.abs(distance)
    inner = (
        3.0 - 2.0 * magnitude + jnp.sqrt(1.0 + 4.0 * magnitude - 4.0 * magnitude * magnitude)
    ) / 8.0
    outer = (
        5.0 - 2.0 * magnitude - jnp.sqrt(-7.0 + 12.0 * magnitude - 4.0 * magnitude * magnitude)
    ) / 8.0
    return jnp.where(magnitude < 1.0, inner, outer)


def stencil_matrix(cells, offsets, first_row, rows):
    line = lax.broadcasted_iota(jnp.int32, (rows, cells.shape[0]), 0)
    relative = cells - first_row
    matrix = jnp.zeros((rows, cells.shape[0]), jnp.float32)
    for shift_value in OFFSETS:
        weight_row = peskin_weight(shift_value - offsets)
        matrix = matrix + jnp.where(
            line == relative[None, :] + shift_value, weight_row[None, :], 0.0
        )
    return matrix


def slot_matrices(group, x_first, y_first, x_rows, y_rows, depth):
    flat = jnp.moveaxis(group, 1, 0).reshape(group.shape[1], -1)
    cells = flat[0:3].astype(jnp.int32)
    x_matrix = stencil_matrix(cells[0], flat[3], x_first, x_rows)
    y_matrix = stencil_matrix(cells[1], flat[4], y_first, y_rows).astype(jnp.bfloat16)
    z_matrix = stencil_matrix(cells[2], flat[5], 0, depth)
    return (flat[6:9], x_matrix, y_matrix, z_matrix)


def fold_ghosts(padded, axis, size):
    core = lax.slice_in_dim(padded, 4, size + 4, axis=axis)
    low_part = lax.slice_in_dim(padded, 0, 2, axis=axis)
    high_part = lax.slice_in_dim(padded, size + 6, size + 8, axis=axis)
    head = lax.slice_in_dim(core, 0, 2, axis=axis) + low_part
    middle = lax.slice_in_dim(core, 2, size - 2, axis=axis)
    tail = lax.slice_in_dim(core, size - 2, size, axis=axis) + high_part
    return jnp.concatenate([head, middle, tail], axis=axis)


def relax(padded_field, padded_visc):
    center_field = padded_field[:, :, 1:-1, 1:-1]
    center_visc = padded_visc[:, :, 1:-1, 1:-1]

    def face(neighbor_field, neighbor_visc):
        return 0.5 * (center_visc + neighbor_visc) * (neighbor_field - center_field)

    total = face(padded_field[:, :, :-2, 1:-1], padded_visc[:, :, :-2, 1:-1])
    total = total + face(padded_field[:, :, 2:, 1:-1], padded_visc[:, :, 2:, 1:-1])
    total = total + face(padded_field[:, :, 1:-1, :-2], padded_visc[:, :, 1:-1, :-2])
    total = total + face(padded_field[:, :, 1:-1, 2:], padded_visc[:, :, 1:-1, 2:])
    vertical = center_field[:, 1:] - center_field[:, :-1]
    vertical = 0.5 * (center_visc[:, 1:] + center_visc[:, :-1]) * vertical
    zeros_layer = jnp.zeros_like(vertical[:, :1])
    z_term = jnp.concatenate([vertical, zeros_layer], axis=1) - jnp.concatenate(
        [zeros_layer, vertical], axis=1
    )
    return center_field + (total + z_term)


def body(velocity, viscosity, marker_cells, marker_offset, marker_force):
    depth = velocity.shape[1]
    width_x = velocity.shape[2]
    width_y = velocity.shape[3]
    markers = marker_cells.shape[2]
    column_size = lax.axis_size("gy")
    my_row = lax.axis_index("gy")
    x_first = lax.axis_index("gx") * width_x - 2
    y_first = my_row * width_y - 2
    packed = jnp.concatenate(
        [marker_cells.astype(jnp.float32), marker_offset, marker_force], axis=1
    )
    slots = column_size * CAP
    column = lax.all_gather(packed, "gy", axis=0, tiled=True)
    owner_row = column[:, 1, 0].astype(jnp.int32) // width_y
    is_mine = owner_row == my_row
    chosen = jnp.argsort(jnp.where(is_mine, 0, 1), stable=True)[:slots]
    kept_flag = is_mine[chosen].astype(jnp.float32)
    received = column[chosen] * kept_flag[:, None, None]
    grouped = received.reshape(-1, group_slots, received.shape[1], markers)
    x_rows = width_x + 4
    y_rows = width_y + 4

    def spread_group(total, group):
        forces, x_matrix, y_matrix, z_matrix = slot_matrices(
            group, x_first, y_first, x_rows, y_rows, depth
        )
        lifted = (
            forces[:, None, None, :] * z_matrix[None, :, None, :] * x_matrix[None, None, :, :]
        ).astype(jnp.bfloat16)
        lifted = lifted.reshape(-1, lifted.shape[-1])
        product = lax.dot_general(
            lifted, y_matrix, (((1,), (1,)), ((), ())), preferred_element_type=jnp.float32
        )
        return (total + product, None)

    spread_init = jnp.zeros((3 * depth * x_rows, y_rows), jnp.float32)
    spread_sum, _ = lax.scan(spread_group, spread_init, grouped)
    force_padded = spread_sum.reshape(3, depth, x_rows, y_rows)
    gathered_ghosts = padded_2(force_padded, (("gx", 2), ("gy", 3)), 2)
    force_field = fold_ghosts(fold_ghosts(gathered_ghosts, 2, width_x), 3, width_y)
    lifted_visc = viscosity[None]
    padded_field, padded_visc = (
        padded_2(velocity, (("gx", 2), ("gy", 3)), 1),
        padded_2(lifted_visc, (("gx", 2), ("gy", 3)), 1),
    )
    first_field = relax(padded_field, padded_visc)
    refreshed = padded_2(first_field, (("gx", 2), ("gy", 3)), 1)
    second_field = relax(refreshed, padded_visc)
    final_field = second_field + force_field
    rim_field = padded_2(final_field.astype(jnp.bfloat16), (("gx", 2), ("gy", 3)), 2)
    rounded_flat = rim_field.reshape(-1, y_rows)

    def sample_group(carry, group):
        unused_forces, x_matrix, y_matrix, z_matrix = slot_matrices(
            group, x_first, y_first, x_rows, y_rows, depth
        )
        along_y = jnp.dot(rounded_flat, y_matrix, preferred_element_type=jnp.float32)
        along_y = along_y.reshape(3, depth, x_rows, -1)
        values = jnp.sum(
            along_y * z_matrix[None, :, None, :] * x_matrix[None, None, :, :], axis=(1, 2)
        )
        return (carry, jnp.moveaxis(values.reshape(3, group_slots, markers), 0, 1))

    _, sampled = lax.scan(sample_group, jnp.zeros((), jnp.float32), grouped)
    sampled = sampled.reshape(slots, 3, markers)
    spread_back = (
        jnp.zeros((column.shape[0], 3, markers), jnp.float32)
        .at[chosen]
        .add(sampled * kept_flag[:, None, None])
    )
    marker_velocity = lax.psum_scatter(spread_back, "gy", scatter_dimension=0, tiled=True)
    return (final_field, marker_velocity)


def solution(mesh):
    in_specs = (
        P(None, None, "gx", "gy"),
        P(None, "gx", "gy"),
        P(("gx", "gy"), None, None),
        P(("gx", "gy"), None, None),
        P(("gx", "gy"), None, None),
    )
    out_specs = (P(None, None, "gx", "gy"), P(("gx", "gy"), None, None))
    return jax.shard_map(body, mesh=mesh, in_specs=in_specs, out_specs=out_specs, check_vma=False)
```

profile of v0, /device:TPU:1, one launch (start us, length us, event | category | flops | bytes accessed | tf_op | source)
XLA Modules:
  0.0 852.9 jit_solution(3252362983962150139)
XLA Ops:
  10.8 4.7 collective-permute-start.3
  16.6 3.6 collective-permute-start.2
  22.1 2.8 collective-permute-done
  26.0 3.8 collective-permute-start.4
  33.1 4.8 collective-permute-start.7
  52.5 28.9 %all-gather.2.cloned.1.call-done = f32[1024,9,128]{2,0,1:T(8,128)} async-done(((f32[32,9,128]{2,0,1:T(8,128)}), f32[1024,9,128]{2,0,1:T(8,128)}) %all-gather.2.cloned.1.call-update) | async-done | bytes 4718608 | tf_op jit(solution)/shard_map/all_gather | solution.py:101
  82.7 4.4 sort.17
  87.0 8.6 %copy.27 = f32[1024,9,128]{2,1,0:T(8,128)} copy(f32[1024,9,128]{2,0,1:T(8,128)} %all-gather.2.cloned.1.call-done) | data formatting | bytes 9437184 | tf_op jit(solution)/shard_map/all_gather | solution.py:101
  95.6 4.0 gather_fusion
  101.4 98.2 %while.22 = (s32[]{:T(128)}, f32[1920,132]{0,1:T(8,128)S(1)}, f32[16,4,9,128]{3,1,2,0:T(4,128)}, s32[]{:T(128)}, s32[]{:T(128)}, /*index=5*/s32[]{:T(128)}, s32[]{:T(128)}) while((s32[]{:T(128)}, f32[1920,132]{0,1:T(8,128)S(1)}, f32[16,4,9,128]{3,1,2,0:T(4,128)}, s32[]{:T(128)}, s32[]{:T(128)}, /*index=5*/s32[]{:T(128)}, ...), condition=%wide.region_2.3_spmd.clone, body=%wide.region_1.2_spmd.clone.sunk | while | flops 263266304 | bytes 10688619 | solution.py:125
  233.5 3.1 pad_maximum_fusion.1
  251.6 3.9 collective-permute-done.16
  256.5 8.9 %collective-permute-start.19 = (bf16[3,32,20,2]{1,3,2,0:T(2,128)(2,1)S(1)}, bf16[3,32,20,2]{1,3,2,0:T(2,128)(2,1)S(1)}, u32[]{:S(2)}, u32[]{:S(2)}) collective-permute-start(bf16[3,32,20,2]{1,3,2,0:T(2,128)(2,1)S(1)} %copy.35), channel_id=1, source_target_pairs={{1,0},{2,1},{3,2},{4,3},{5,4},{6,5},{7,6},{8,7},{9,8},{10,9},{11,1... | collective-permute-start | bytes 23048 | tf_op jit(solution)/shard_map/ppermute | solution.py:21
  266.8 3.1 collective-permute-done.18
  272.0 275.1 %while.21 = (s32[]{:T(128)}, f32[16,4,3,128]{3,2,1,0:T(4,128)S(1)}, f32[16,4,9,128]{3,1,2,0:T(4,128)}, s32[]{:T(128)}, bf16[1920,132]{1,0:T(8,128)(2,1)S(1)}, /*index=5*/s32[]{:T(128)}, s32[]{:T(128)}) while((s32[]{:T(128)}, f32[16,4,3,128]{3,2,1,0:T(4,128)S(1)}, f32[16,4,9,128]{3,1,2,0:T(4,128)}, s32[]{:T(128)}, ...), condition=%wide.region_5.6_spmd, body=%wide.region_3.5_spmd.sunk | while | flops 263691776 | bytes 24585316 | solution.py:152
  275.6 5.6 copy.51
  281.2 4.9 reshape.1370
  286.2 3.0 multiply_reduce_fusion.2
  292.8 5.6 copy.51
  298.4 4.9 reshape.1370
  303.4 3.0 multiply_reduce_fusion.2
  310.0 5.6 copy.51
  315.5 4.9 reshape.1370
  320.6 3.0 multiply_reduce_fusion.2
  327.2 5.6 copy.51
  332.7 4.9 reshape.1370
  337.8 3.0 multiply_reduce_fusion.2
  344.4 5.6 copy.51
  349.9 4.9 reshape.1370
  355.0 3.0 multiply_reduce_fusion.2
  361.6 5.6 copy.51
  367.1 4.9 reshape.1370
  372.2 3.0 multiply_reduce_fusion.2
  378.8 5.6 copy.51
  384.3 4.9 reshape.1370
  389.4 3.0 multiply_reduce_fusion.2
  396.0 5.6 copy.51
  401.5 4.9 reshape.1370
  406.6 3.0 multiply_reduce_fusion.2
  413.2 5.6 copy.51
  418.7 4.9 reshape.1370
  423.8 3.0 multiply_reduce_fusion.2
  430.4 5.6 copy.51
  435.9 4.9 reshape.1370
  440.9 3.0 multiply_reduce_fusion.2
  447.6 5.6 copy.51
  453.1 4.9 reshape.1370
  458.1 3.0 multiply_reduce_fusion.2
  464.8 5.6 copy.51
  470.3 4.9 reshape.1370
  475.3 3.0 multiply_reduce_fusion.2
  481.9 5.6 copy.51
  487.5 4.9 reshape.1370
  492.5 3.0 multiply_reduce_fusion.2
  499.1 5.6 copy.51
  504.7 4.9 reshape.1370
  509.7 3.0 multiply_reduce_fusion.2
  516.3 5.6 copy.51
  521.9 4.9 reshape.1370
  526.9 3.0 multiply_reduce_fusion.2
  533.5 5.6 copy.51
  539.1 4.9 reshape.1370
  544.1 3.0 multiply_reduce_fusion.2
  553.0 291.4 %all-reduce.7.cloned.1.call-done = f32[1024,3,128]{2,1,0:T(4,128)} async-done(((f32[1024,3,128]{2,1,0:T(4,128)}), f32[1024,3,128]{2,1,0:T(4,128)}) %all-reduce.7.cloned.1.call-update) | async-done | bytes 1572880
  (584 shorter events, 243.3 us)
Async XLA Ops:
  7.2 14.2 %copy-start.4 = (f32[3,32,16,128]{3,2,1,0:T(8,128)S(1)}, f32[3,32,16,128]{3,2,1,0:T(8,128)}, u32[]{:S(2)}) copy-start(f32[3,32,16,128]{3,2,1,0:T(8,128)} %param.9) | copy-start | bytes 2359300
  7.2 74.2 %all-gather.2.cloned.1.call-start = ((), (), s32[]{:S(2)}) async-start(), calls=%async_computation | async-start | bytes 4866048 | tf_op jit(solution)/shard_map/all_gather | solution.py:101
  9.6 834.8 %all-reduce.7.cloned.1.call-start = ((), (), s32[]{:S(2)}) async-start(), calls=%async_computation.1 | async-start | bytes 4194304
  10.8 19.0 %collective-permute-start.3 = (f32[3,32,1,128]{3,2,1,0:T(1,128)S(1)}, f32[3,32,1,128]{3,2,1,0:T(1,128)S(1)}, u32[]{:S(2)}, u32[]{:S(2)}) collective-permute-start(f32[3,32,1,128]{3,2,1,0:T(1,128)S(1)} %get-tuple-element.206), channel_id=1, source_target_pairs={{32,0},{64,32},{96,64},{128,96},{160,128},{192,160},{224,192},{0,2... | collective-permute-start | bytes 147464 | tf_op jit(solution)/shard_map/ppermute | solution.py:21
  15.6 14.3 %collective-permute-start.1 = (f32[3,32,1,128]{3,2,1,0:T(1,128)S(1)}, f32[3,32,1,128]{3,2,1,0:T(1,128)S(1)}, u32[]{:S(2)}, u32[]{:S(2)}) collective-permute-start(f32[3,32,1,128]{3,2,1,0:T(1,128)S(1)} %get-tuple-element.205), channel_id=1, source_target_pairs={{0,32},{32,64},{64,96},{96,128},{128,160},{160,192},{192,224},{224... | collective-permute-start | bytes 147464 | tf_op jit(solution)/shard_map/ppermute | solution.py:20
  16.6 4.9 collective-permute-start.2
  20.2 4.7 copy-start.10
  20.2 4.7 collective-permute-start
  21.4 0.7 copy-start.16
  26.0 12.5 %collective-permute-start.4 = (f32[1,32,18,1]{3,2,1,0:T(8,128)}, f32[1,32,18,1]{3,2,1,0:T(8,128)S(1)}, u32[]{:S(2)}, u32[]{:S(2)}) collective-permute-start(f32[1,32,18,1]{3,2,1,0:T(8,128)} %get-tuple-element.211), channel_id=1, source_target_pairs={{0,1},{1,2},{2,3},{3,4},{4,5},{5,6},{6,7},{7,8},{8,9},{9,10},{10,1... | collective-permute-start | bytes 6920 | tf_op jit(solution)/shard_map/ppermute | solution.py:20
  29.8 8.7 %collective-permute-start.6 = (f32[1,32,18,1]{3,2,1,0:T(8,128)}, f32[1,32,18,1]{3,2,1,0:T(8,128)}, u32[]{:S(2)}, u32[]{:S(2)}) collective-permute-start(f32[1,32,18,1]{3,2,1,0:T(8,128)} %get-tuple-element.212), channel_id=1, source_target_pairs={{1,0},{2,1},{3,2},{4,3},{5,4},{6,5},{7,6},{8,7},{9,8},{10,9},{11,1... | collective-permute-start | bytes 6920 | tf_op jit(solution)/shard_map/ppermute | solution.py:21
  29.8 1.6 copy-start.22
  29.8 1.6 copy-start.23
  33.1 7.7 collective-permute-start.7
  38.4 2.9 collective-permute-start.5
  45.5 35.8 %copy-start = (f32[3,32,16,128]{3,2,1,0:T(8,128)}, f32[3,32,16,128]{3,2,1,0:T(8,128)S(1)}, u32[]{:S(2)}) copy-start(f32[3,32,16,128]{3,2,1,0:T(8,128)S(1)} %fusion.220) | copy-start | bytes 2359300
  45.6 3.3 collective-permute-start.9
  45.8 5.5 collective-permute-start.8
  49.0 46.7 %copy-start.18 = (f32[3,32,1,128]{3,2,1,0:T(1,128)}, f32[3,32,1,128]{3,2,1,0:T(1,128)S(1)}, u32[]{:S(2)}) copy-start(f32[3,32,1,128]{3,2,1,0:T(1,128)S(1)} %collective-permute-done.9) | copy-start | bytes 147460
  51.3 44.3 %copy-start.20 = (f32[3,32,1,128]{3,2,1,0:T(1,128)}, f32[3,32,1,128]{3,2,1,0:T(1,128)S(1)}, u32[]{:S(2)}) copy-start(f32[3,32,1,128]{3,2,1,0:T(1,128)S(1)} %collective-permute-done.8) | copy-start | bytes 147460
  201.5 4.3 copy-start.5
  204.1 8.6 %collective-permute-start.13 = (f32[3,32,2,132]{3,2,1,0:T(2,128)}, f32[3,32,2,132]{3,2,1,0:T(2,128)}, u32[]{:S(2)}, u32[]{:S(2)}) collective-permute-start(f32[3,32,2,132]{3,2,1,0:T(2,128)} %get-tuple-element.196), channel_id=1, source_target_pairs={{32,0},{64,32},{96,64},{128,96},{160,128},{192,160},{224,192},{0,2... | collective-permute-start | bytes 304136 | tf_op jit(solution)/shard_map/ppermute | solution.py:21
  205.8 8.4 collective-permute-start.12
  207.6 2.9 copy-start.9
  210.0 15.0 %collective-permute-start.11 = (f32[3,32,18,1]{1,3,2,0:T(1,128)}, f32[3,32,18,1]{1,3,2,0:T(1,128)}, u32[]{:S(2)}, u32[]{:S(2)}) collective-permute-start(f32[3,32,18,1]{1,3,2,0:T(1,128)} %copy.25), channel_id=1, source_target_pairs={{1,0},{2,1},{3,2},{4,3},{5,4},{6,5},{7,6},{8,7},{9,8},{10,9},{11,1... | collective-permute-start | bytes 20744 | tf_op jit(solution)/shard_map/ppermute | solution.py:21
  211.5 15.7 %collective-permute-start.10 = (f32[3,32,18,1]{1,3,2,0:T(1,128)}, f32[3,32,18,1]{1,3,2,0:T(1,128)}, u32[]{:S(2)}, u32[]{:S(2)}) collective-permute-start(f32[3,32,18,1]{1,3,2,0:T(1,128)} %copy.23), channel_id=1, source_target_pairs={{0,1},{1,2},{2,3},{3,4},{4,5},{5,6},{6,7},{7,8},{8,9},{9,10},{10,1... | collective-permute-start | bytes 20744 | tf_op jit(solution)/shard_map/ppermute | solution.py:20
  217.5 6.6 copy-start.1
  217.5 6.6 copy-start.17
  219.3 10.2 %collective-permute-start.15 = (f32[3,32,24,2]{1,2,3,0:T(8,128)S(1)}, f32[3,32,24,2]{1,2,3,0:T(8,128)S(1)}, u32[]{:S(2)}, u32[]{:S(2)}) collective-permute-start(f32[3,32,24,2]{1,2,3,0:T(8,128)S(1)} %copy.31), channel_id=1, source_target_pairs={{1,0},{2,1},{3,2},{4,3},{5,4},{6,5},{7,6},{8,7},{9,8},{10,9},{11,1... | collective-permute-start | bytes 55304 | tf_op jit(solution)/shard_map/ppermute | solution.py:21
  223.3 7.8 collective-permute-start.14
  236.7 1.3 copy-start.2
  236.7 1.6 copy-start.3
  243.1 1.3 copy-start.8
  243.1 1.5 copy-start.11
  243.1 1.5 copy-start.13
  243.1 1.6 copy-start.14
  243.1 1.6 copy-start.15
  243.8 1.6 copy-start.7
  243.8 1.6 copy-start.12
  243.8 1.6 copy-start.19
  243.9 1.6 copy-start.21
  247.8 3.8 collective-permute-start.17
  250.4 5.0 collective-permute-start.16
  256.5 9.8 %collective-permute-start.19 = (bf16[3,32,20,2]{1,3,2,0:T(2,128)(2,1)S(1)}, bf16[3,32,20,2]{1,3,2,0:T(2,128)(2,1)S(1)}, u32[]{:S(2)}, u32[]{:S(2)}) collective-permute-start(bf16[3,32,20,2]{1,3,2,0:T(2,128)(2,1)S(1)} %copy.35), channel_id=1, source_target_pairs={{1,0},{2,1},{3,2},{4,3},{5,4},{6,5},{7,6},{8,7},{9,8},{10,9},{11,1... | collective-permute-start | bytes 23048 | tf_op jit(solution)/shard_map/ppermute | solution.py:21
  265.9 4.0 collective-permute-start.18
  547.6 4.1 copy-start.24
  550.3 1.4 copy-start.6
Sparse Core Ops, SparseCore 0:
  10.6 70.7 all-gather.1
  551.8 292.4 all-reduce.6
where the time goes:
time: 867 us; the launch traced here: 853 us
  waiting for transfers between devices  337 us (39%)
  local copies, waits for them, and re-layouts  279 us (32%)
  other arithmetic  99.6 us (11%)
  matrix products  82.7 us (10%)
  starting transfers between devices  36.6 us (4%)
  between operations  15.4 us (2%)
    unnamed x3, waiting for transfers between devices  291 us
    dot_general x16, local copies, waits for them, and re-layouts, sample_group(): jnp.dot(rounded_flat, y_matrix, preferred_element_type=jnp.float32)  88.9 us
    reshape x16, local copies, waits for them, and re-layouts, sample_group(): along_y = along_y.reshape(3, depth, x_rows, -1)  77.9 us
    reduce_sum x16, other arithmetic, sample_group(): jnp.sum(along_y * z_matrix[None, :, None, :] * x_matrix[None, None, :, :]...  48.3 us
    dot_general x16, matrix products, sample_group(): jnp.dot(rounded_flat, y_matrix, preferred_element_type=jnp.float32)  43.1 us
    dot_general x16, matrix products, spread_group(): lax.dot_general(lifted, y_matrix, (((1,), (1,)), ((), ())), preferred_ele...  39.6 us
    convert_element_type x16, local copies, waits for them, and re-layouts, spread_group(): lifted = (forces[:, None, None, :] * z_matrix[None, :, None, :] * x_matri...  31.8 us
    all_gather x1, waiting for transfers between devices, body(): column = lax.all_gather(packed, 'gy', axis=0, tiled=True)  28.9 us
  transfers between devices with their start and end apart: 22, of which 11 were waited for; matrix products, arithmetic and copies ran while one was open for 4% of the time, Pallas kernels for 0%

commit v1 on v0

v1 whole, which is shorter than its diff:
```python
import jax
import jax.numpy as jnp
from jax import lax
from jax.experimental import pallas as pl
from jax.experimental.pallas import tpu as pltpu
from jax.sharding import PartitionSpec as P

CAP = 2
OFFSETS = (-1, 0, 1, 2)
GROUP = 8
XR = 19
YR = 144


def peskin_weight(distance):
    magnitude = jnp.abs(distance)
    inner = (
        3.0 - 2.0 * magnitude + jnp.sqrt(1.0 + 4.0 * magnitude - 4.0 * magnitude * magnitude)
    ) / 8.0
    outer = (
        5.0 - 2.0 * magnitude - jnp.sqrt(-7.0 + 12.0 * magnitude - 4.0 * magnitude * magnitude)
    ) / 8.0
    return jnp.where(magnitude < 1.0, inner, outer)


def stencil_rows(rows, cell, weights, direction, slot, wrap):
    line = lax.broadcasted_iota(jnp.int32, (rows, cell.shape[1]), 0)
    matrix = jnp.zeros((rows, cell.shape[1]), jnp.float32)
    for place, shift in enumerate(OFFSETS):
        target = cell + shift
        if wrap:
            target = jnp.where(target < 0, rows - 1, target)
        matrix = jnp.where(
            line == target, weights[4 * direction + place, slot : slot + 1, :], matrix
        )
    return matrix


def spread_kernel(cells, weights, forces, total, y_out, x_out, z_out, lifted):
    depth = z_out.shape[1]
    markers = cells.shape[2]

    @pl.when(pl.program_id(0) == 0)
    def _():
        total[...] = jnp.zeros_like(total)

    for slot in range(GROUP):
        lanes = slice(slot * markers, (slot + 1) * markers)
        one = slice(slot, slot + 1)
        y_matrix = stencil_rows(YR, cells[1, one, :], weights, 1, slot, True)
        y_out[0, :, lanes] = y_matrix.astype(jnp.bfloat16)
        x_out[0, :, lanes] = stencil_rows(24, cells[0, one, :] + 1, weights, 0, slot, False)
        z_out[0, :, lanes] = stencil_rows(depth, cells[2, one, :], weights, 2, slot, False)
    for comp in range(3):
        for slot in range(GROUP):
            lanes = slice(slot * markers, (slot + 1) * markers)
            scaled = forces[comp, slot : slot + 1, :] * z_out[0, :, lanes]
            for x in range(XR):
                lifted[x * depth : (x + 1) * depth, lanes] = (
                    scaled * x_out[0, x : x + 1, lanes]
                ).astype(jnp.bfloat16)
        total[comp] += lax.dot_general(
            lifted[...], y_out[0], (((1,), (1,)), ((), ())), preferred_element_type=jnp.float32
        )


def sample_kernel(field, y_ref, x_ref, z_ref, out):
    depth = z_ref.shape[1]
    for comp in range(3):
        along_y = jnp.dot(field[comp], y_ref[0], preferred_element_type=jnp.float32)
        column = along_y[0:depth] * x_ref[0, 0:1, :]
        for x in range(1, XR):
            column = column + along_y[x * depth : (x + 1) * depth] * x_ref[0, x : x + 1, :]
        out[0, comp : comp + 1, :] = jnp.sum(column * z_ref[0], axis=0, keepdims=True)


def exchange(array, axis, dim, low_width, high_width):
    count, length = lax.axis_size(axis), array.shape[dim]
    up = [(i, (i + 1) % count) for i in range(count)]
    down = [(j, i) for i, j in up]
    before = lax.ppermute(
        lax.slice_in_dim(array, length - low_width, length, axis=dim), axis, up
    )
    after = lax.ppermute(lax.slice_in_dim(array, 0, high_width, axis=dim), axis, down)
    return before, after


def padded(array, axis, dim, width):
    before, after = exchange(array, axis, dim, width, width)
    return jnp.concatenate([before, array, after], axis=dim)


def relax(field, visc):
    center_field = field[:, 1:-1, :, 1:-1]
    center_visc = visc[:, 1:-1, :, 1:-1]

    def face(neighbor_field, neighbor_visc):
        return 0.5 * (center_visc + neighbor_visc) * (neighbor_field - center_field)

    total = face(field[:, :-2, :, 1:-1], visc[:, :-2, :, 1:-1])
    total = total + face(field[:, 2:, :, 1:-1], visc[:, 2:, :, 1:-1])
    total = total + face(field[:, 1:-1, :, :-2], visc[:, 1:-1, :, :-2])
    total = total + face(field[:, 1:-1, :, 2:], visc[:, 1:-1, :, 2:])
    vertical = center_field[:, :, 1:] - center_field[:, :, :-1]
    vertical = 0.5 * (center_visc[:, :, 1:] + center_visc[:, :, :-1]) * vertical
    zeros_layer = jnp.zeros_like(vertical[:, :, :1])
    z_term = jnp.concatenate([vertical, zeros_layer], axis=2) - jnp.concatenate(
        [zeros_layer, vertical], axis=2
    )
    return center_field + (total + z_term)


def body(velocity, viscosity, marker_cells, marker_offset, marker_force):
    depth, width_x, width_y = velocity.shape[1:]
    blocks, _, markers = marker_cells.shape
    column_size = lax.axis_size("gy")
    slots = column_size * CAP
    steps = slots // GROUP

    target = marker_cells[:, 1, 0] // width_y
    same = target[:, None] == target[None, :]
    earlier = jnp.tril(jnp.ones((blocks, blocks), jnp.bool_), -1)
    rank = jnp.sum(jnp.where(same & earlier, 1, 0), axis=1)
    slot_of = target * CAP + rank
    place = (lax.broadcasted_iota(jnp.int32, (slots, blocks), 0) == slot_of[None, :]).astype(
        jnp.float32
    )
    local = jnp.stack(
        [
            marker_cells[:, 0] - lax.axis_index("gx") * width_x,
            marker_cells[:, 1] - target[:, None] * width_y,
            marker_cells[:, 2],
        ],
        axis=1,
    )
    packed = jnp.concatenate([local.astype(jnp.float32), marker_offset, marker_force], axis=1)
    sent = jnp.dot(place, packed.reshape(blocks, -1), precision=lax.Precision.HIGHEST)
    sent = sent.reshape(column_size, CAP * 9, markers)
    received = lax.all_to_all(sent, "gy", 0, 0, tiled=True)
    received = jnp.moveaxis(received.reshape(slots, 9, markers), 1, 0)
    cells = received[0:3].astype(jnp.int32)
    weights = jnp.stack(
        [peskin_weight(shift - received[3 + d]) for d in range(3) for shift in OFFSETS]
    )
    forces = received[6:9]

    rows = XR * depth
    lanes = GROUP * markers
    total, y_matrix, x_matrix, z_matrix = pl.pallas_call(
        spread_kernel,
        grid=(steps,),
        in_specs=[
            pl.BlockSpec((3, GROUP, markers), lambda g: (0, g, 0)),
            pl.BlockSpec((12, GROUP, markers), lambda g: (0, g, 0)),
            pl.BlockSpec((3, GROUP, markers), lambda g: (0, g, 0)),
        ],
        out_specs=[
            pl.BlockSpec((3, rows, YR), lambda g: (0, 0, 0)),
            pl.BlockSpec((1, YR, lanes), lambda g: (g, 0, 0)),
            pl.BlockSpec((1, 24, lanes), lambda g: (g, 0, 0)),
            pl.BlockSpec((1, depth, lanes), lambda g: (g, 0, 0)),
        ],
        out_shape=[
            jax.ShapeDtypeStruct((3, rows, YR), jnp.float32),
            jax.ShapeDtypeStruct((steps, YR, lanes), jnp.bfloat16),
            jax.ShapeDtypeStruct((steps, 24, lanes), jnp.float32),
            jax.ShapeDtypeStruct((steps, depth, lanes), jnp.float32),
        ],
        scratch_shapes=[pltpu.VMEM((rows, lanes), jnp.bfloat16)],
        name="spread",
    )(cells, weights, forces)

    stacked = jnp.concatenate([velocity, viscosity[None]], axis=0)
    stacked = jnp.swapaxes(stacked, 1, 2)
    stacked = padded(padded(stacked, "gx", 1, 2), "gy", 3, 2)
    visc = stacked[3:4]
    first = relax(stacked[0:3], visc)
    second = relax(first, visc[:, 1:-1, :, 1:-1])

    total = total.reshape(3, XR, depth, YR)
    count_x, count_y = lax.axis_size("gx"), lax.axis_size("gy")
    up_x = [(i, (i + 1) % count_x) for i in range(count_x)]
    down_x = [(j, i) for i, j in up_x]
    up_y = [(i, (i + 1) % count_y) for i in range(count_y)]
    down_y = [(j, i) for i, j in up_y]
    from_low = lax.ppermute(total[:, width_x + 1 :], "gx", up_x)
    from_high = lax.ppermute(total[:, 0:1], "gx", down_x)
    core = total[:, 1 : width_x + 1]
    core = core + jnp.pad(from_low, ((0, 0), (0, width_x - 2), (0, 0), (0, 0)))
    core = core + jnp.pad(from_high, ((0, 0), (width_x - 1, 0), (0, 0), (0, 0)))
    from_low = lax.ppermute(core[..., width_y : width_y + 2], "gy", up_y)
    from_high = lax.ppermute(core[..., YR - 1 :], "gy", down_y)
    force = core[..., :width_y]
    force = force + jnp.pad(from_low, ((0, 0), (0, 0), (0, 0), (0, width_y - 2)))
    force = force + jnp.pad(from_high, ((0, 0), (0, 0), (0, 0), (width_y - 1, 0)))
    final = second + force

    rounded = final.astype(jnp.bfloat16)
    before, after = exchange(rounded, "gx", 1, 1, 2)
    rounded = jnp.concatenate([before, rounded, after], axis=1)
    before, after = exchange(rounded, "gy", 3, 1, 2)
    middle = jnp.zeros((3, XR, depth, YR - width_y - 3), jnp.bfloat16)
    field = jnp.concatenate([rounded, after, middle, before], axis=3).reshape(3, rows, YR)

    sampled = pl.pallas_call(
        sample_kernel,
        grid=(steps,),
        in_specs=[
            pl.BlockSpec((3, rows, YR), lambda g: (0, 0, 0)),
            pl.BlockSpec((1, YR, lanes), lambda g: (g, 0, 0)),
            pl.BlockSpec((1, 24, lanes), lambda g: (g, 0, 0)),
            pl.BlockSpec((1, depth, lanes), lambda g: (g, 0, 0)),
        ],
        out_specs=pl.BlockSpec((1, 3, lanes), lambda g: (g, 0, 0)),
        out_shape=jax.ShapeDtypeStruct((steps, 3, lanes), jnp.float32),
        name="sample",
    )(field, y_matrix, x_matrix, z_matrix)
    sampled = jnp.swapaxes(sampled.reshape(steps, 3, GROUP, markers), 1, 2)
    sampled = sampled.reshape(column_size, CAP * 3, markers)
    returned = lax.all_to_all(sampled, "gy", 0, 0, tiled=True).reshape(slots, -1)
    marker_velocity = jnp.dot(place.T, returned, precision=lax.Precision.HIGHEST)
    return (jnp.swapaxes(final, 1, 2), marker_velocity.reshape(blocks, 3, markers))


def solution(mesh):
    in_specs = (
        P(None, None, "gx", "gy"),
        P(None, "gx", "gy"),
        P(("gx", "gy"), None, None),
        P(("gx", "gy"), None, None),
        P(("gx", "gy"), None, None),
    )
    out_specs = (P(None, None, "gx", "gy"), P(("gx", "gy"), None, None))
    return jax.shard_map(body, mesh=mesh, in_specs=in_specs, out_specs=out_specs, check_vma=False)
```

time: 867 us -> 153 us (0.18); the launches traced: 853 us -> 152 us
  waiting for transfers between devices: 337 us -> 22.9 us
  local copies, waits for them, and re-layouts: 279 us -> 23.9 us
  matrix products: 82.7 us -> 1.23 us
  other arithmetic: 99.6 us -> 23 us
  Pallas kernels: 0 us -> 28.3 us
  starting transfers between devices: 36.6 us -> 51.6 us
  between operations: 15.4 us -> 1.04 us
    unnamed x3 -> x0, waiting for transfers between devices: 291 us -> none
    dot_general x16 -> x0, local copies, waits for them, and re-layouts: 88.9 us -> none  [sample_group(): jnp.dot(rounded_flat, y_matrix, preferred_element_type=jnp.float32)]
    dot_general x32 -> x2, matrix products: 82.7 us -> 1.23 us  [the longest x1 0.84 us: body(): jnp.dot(place.T, returned, precision=lax.Precision.HIGHEST)]
    reshape x18 -> x6, local copies, waits for them, and re-layouts: 80.1 us -> 2.65 us  [the longest x1 0.97 us: body(): sampled = jnp.swapaxes(sampled.reshape(steps, 3, GROUP, markers), 1, 2)]
    reduce_sum x16 -> x1, other arithmetic: 48.3 us -> 0.18 us  [body(): rank = jnp.sum(jnp.where(same & earlier, 1, 0), axis=1)]
    convert_element_type x17 -> x0, local copies, waits for them, and re-layouts: 31.9 us -> none  [the longest x16 31.8 us: spread_group(): lifted = (forces[:, None, None, :] * z_matrix[None, :, None, :] * x_matri...]
    all_gather x1 -> x0, waiting for transfers between devices: 28.9 us -> none  [body(): column = lax.all_gather(packed, 'gy', axis=0, tiled=True)]
    pallas_call x0 -> x2, Pallas kernels: none -> 28.3 us  [the longest x1 16.9 us: body(): pl.pallas_call(spread_kernel, grid=(steps,), in_specs=[pl.BlockSpec((3, G...]
  transfers between devices with their start and end apart: 22 -> 14, of which waited for: 11 -> 5; matrix products, arithmetic and copies ran while one was open for 4% -> 17% of each run, Pallas kernels for 0% -> 0%
where the time goes in v1:
time: 153 us; the launch traced here: 152 us
  starting transfers between devices  51.6 us (34%)
  Pallas kernels  28.3 us (18%)
  local copies, waits for them, and re-layouts  23.9 us (16%)
  other arithmetic  23 us (15%)
  waiting for transfers between devices  22.9 us (15%)
    pallas_call x1, Pallas kernels, body(): pl.pallas_call(spread_kernel, grid=(steps,), in_specs=[pl.BlockSpec((3, G...  16.9 us
    ppermute x4, starting transfers between devices, exchange(): lax.ppermute(lax.slice_in_dim(array, 0, high_width, axis=dim), axis, down)  13.3 us
    all_to_all x1, starting transfers between devices, body(): received = lax.all_to_all(sent, 'gy', 0, 0, tiled=True)  12.1 us
    all_to_all x1, starting transfers between devices, body(): lax.all_to_all(sampled, 'gy', 0, 0, tiled=True).reshape(slots, -1)  11.5 us
    pallas_call x1, Pallas kernels, body(): pl.pallas_call(sample_kernel, grid=(steps,), in_specs=[pl.BlockSpec((3, r...  11.4 us
    ppermute x4, waiting for transfers between devices, exchange(): lax.ppermute(lax.slice_in_dim(array, length - low_width, length, axis=dim...  10.4 us
    all_to_all x1, waiting for transfers between devices, body(): lax.all_to_all(sampled, 'gy', 0, 0, tiled=True).reshape(slots, -1)  10 us
    convert_element_type x1, other arithmetic, body(): rounded = final.astype(jnp.bfloat16)  5.76 us
  transfers between devices with their start and end apart: 14, of which 5 were waited for; matrix products, arithmetic and copies ran while one was open for 17% of the time, Pallas kernels for 0%

profile of v1, /device:TPU:1, one launch (start us, length us, event | category | flops | bytes accessed | tf_op | source)
XLA Modules:
  0.0 152.0 jit_solution(7116352314296341986)
XLA Ops:
  0.6 1.4 copy.63
  2.1 1.1 copy.99
  3.2 2.1 %collective-permute-start = (f32[4,2,32,128]{3,2,1,0:T(8,128)S(1)}, f32[4,2,32,128]{3,2,1,0:T(8,128)S(1)}, u32[]{:S(2)}, u32[]{:S(2)}) collective-permute-start(f32[4,2,32,128]{3,2,1,0:T(8,128)S(1)} %get-tuple-element.34), channel_id=1, source_target_pairs={{0,32},{32,64},{64,96},{96,128},{128,160},{160,192},{192,224},{224... | collective-permute-start | bytes 393224 | tf_op jit(solution)/shard_map/ppermute | solution.py:81
  5.4 2.7 %collective-permute-start.1 = (f32[4,2,32,128]{3,2,1,0:T(8,128)S(1)}, f32[4,2,32,128]{3,2,1,0:T(8,128)S(1)}, u32[]{:S(2)}, u32[]{:S(2)}) collective-permute-start(f32[4,2,32,128]{3,2,1,0:T(8,128)S(1)} %get-tuple-element.35), channel_id=1, source_target_pairs={{32,0},{64,32},{96,64},{128,96},{160,128},{192,160},{224,192},{0,2... | collective-permute-start | bytes 393224 | tf_op jit(solution)/shard_map/ppermute | solution.py:84
  8.1 0.1 slice_reduce_fusion
  8.2 0.2 select_reduce_fusion
  8.5 0.4 fusion.45
  8.9 0.8 reshape.117
  9.7 12.1 %all-to-all-start = ((f32[32,18,128]{2,1,0:T(8,128)}), f32[32,18,128]{2,1,0:T(8,128)S(1)}, u32[]{:S(2)}, u32[]{:S(2)}) async-start(f32[32,18,128]{2,1,0:T(8,128)} %reshape.117), calls=%async_computation | async-start | bytes 786432 | tf_op jit(solution)/shard_map/all_to_all | solution.py:139
  21.9 0.1 pad_maximum_fusion.2
  22.0 1.6 %fusion.130 = (f32[4,20,32,2]{3,2,1,0:T(8,128)}, f32[4,20,32,2]{3,2,1,0:T(8,128)S(1)}) fusion(f32[4,20,32,128]{3,2,1,0:T(8,128)S(1)} %pad_maximum_fusion.2), kind=kLoop, calls=%fused_computation.211 | loop fusion | bytes 81920 | tf_op jit(solution)/shard_map/slice | solution.py:82
  23.6 1.9 %copy.64 = f32[4,20,32,2]{2,0,3,1:T(4,128)S(1)} copy(f32[4,20,32,2]{3,2,1,0:T(8,128)} %get-tuple-element.30) | data formatting | bytes 40960 | tf_op jit(solution)/shard_map/slice | solution.py:82
  25.4 1.7 %collective-permute-start.2 = (f32[4,20,32,2]{2,0,3,1:T(4,128)S(1)}, f32[4,20,32,2]{2,0,3,1:T(4,128)S(1)}, u32[]{:S(2)}, u32[]{:S(2)}) collective-permute-start(f32[4,20,32,2]{2,0,3,1:T(4,128)S(1)} %copy.64), channel_id=1, source_target_pairs={{0,1},{1,2},{2,3},{3,4},{4,5},{5,6},{6,7},{7,8},{8,9},{9,10},{10,1... | collective-permute-start | bytes 61448 | tf_op jit(solution)/shard_map/ppermute | solution.py:81
  27.1 0.5 copy.65
  27.7 0.2 collective-permute-start.3
  27.9 0.7 fusion.34
  28.6 1.0 collective-permute-done.2
  29.6 0.5 copy.66
  30.2 2.5 %collective-permute-done.3 = f32[4,20,32,2]{2,0,3,1:T(4,128)S(1)} collective-permute-done((f32[4,20,32,2]{2,0,3,1:T(4,128)S(1)}, f32[4,20,32,2]{2,0,3,1:T(4,128)S(1)}, u32[]{:S(2)}, u32[]{:S(2)}) %collective-permute-start.3) | collective-permute-done | bytes 20512 | tf_op jit(solution)/shard_map/ppermute | solution.py:84
  32.7 1.6 %copy.67 = f32[4,20,32,2]{3,2,1,0:T(8,128)} copy(f32[4,20,32,2]{2,0,3,1:T(4,128)S(1)} %collective-permute-done.3) | data formatting | bytes 40960 | tf_op jit(solution)/shard_map/ppermute | solution.py:84
  34.3 2.4 %pad_maximum_fusion = f32[4,20,32,132]{3,2,1,0:T(8,128)S(1)} fusion(f32[4,20,32,2]{3,2,1,0:T(8,128)} %copy.67, f32[4,2,32,128]{3,2,1,0:T(8,128)S(1)} %collective-permute-done.1, f32[4,16,32,128]{3,2,1,0:T(8,128)S(1)} %maximum_bitcast_fusion, f32[4,2,32,128]{3,2,1,0:T(8,128)S(1)} %collective-permute-done, f32[4,20,32,2]{3,2,1,0:T(8,128)S(1)} %copy.66), kind=kLoop, calls=%fused_computation | loop fusion | flops 1351680 | bytes 2703360 | tf_op jit(solution)/shard_map/concatenate | solution.py:90
  36.7 0.4 fusion.24
  37.1 1.0 fusion
  38.1 0.3 copy-done
  38.4 0.7 fusion.32
  39.1 0.9 maximum_maximum_fusion
  40.0 2.7 %fusion.4 = f32[3,18,32,130]{3,2,1,0:T(8,128)} fusion(f32[4,20,32,130]{3,2,1,0:T(8,128)S(1)} %get-tuple-element.29, f32[4,20,32,130]{3,2,1,0:T(8,128)S(1)} %get-tuple-element.28, f32[4,20,32,132]{3,2,1,0:T(8,128)S(1)} %pad_maximum_fusion, f32[3,18,31,130]{3,2,1,0:T(8,128)S(1)} %fusion, f32[18,32,130]{2,1,0:T(8,128)S(1)} %get-tuple-element.24, ...), kind=kLoop, calls=%fused_computation.9 | loop fusion | flops 3144960 | bytes 7459920 | tf_op jit(solution)/shard_map/add | solution.py:110
  42.8 0.1 copy.98
  42.9 0.7 fusion.132
  44.2 0.7 copy-done.5
  44.9 16.9 %spread.1 = (f32[3,608,144]{2,1,0:T(8,128)}, bf16[8,144,1024]{2,1,0:T(8,128)(2,1)}, f32[8,24,1024]{2,1,0:T(8,128)}, f32[8,32,1024]{2,1,0:T(8,128)}) custom-call(s32[3,64,128]{2,1,0:T(8,128)} %get-tuple-element.37.cells, f32[12,64,128]{2,1,0:T(8,128)} %copy-done.5, f32[3,64,128]{2,1,0:T(8,128)} %get-tuple-element.36.forces), custom_call_target="tpu_custom_call" | custom-call | tf_op jit(solution)/shard_map/spread/pallas_call | solution.py:149
  61.9 1.1 slice.283
  62.9 0.9 slice.284
  63.8 3.6 %collective-permute-start.5 = (f32[3,1,32,144]{3,2,1,0:T(8,128)S(1)}, f32[3,1,32,144]{3,2,1,0:T(8,128)S(1)}, u32[]{:S(2)}, u32[]{:S(2)}) collective-permute-start(f32[3,1,32,144]{3,2,1,0:T(8,128)S(1)} %slice.284), channel_id=1, source_target_pairs={{32,0},{64,32},{96,64},{128,96},{160,128},{192,160},{224,192},{0,2... | collective-permute-start | bytes 165896 | tf_op jit(solution)/shard_map/ppermute | solution.py:187
  67.4 3.2 %fusion.13 = f32[3,16,31,128]{3,2,1,0:T(8,128)} fusion(f32[3,18,32,130]{3,2,1,0:T(8,128)} %fusion.4, f32[16,31,128]{2,1,0:T(8,128)S(1)} %copy-done.4), kind=kLoop, calls=%fused_computation.27 | loop fusion | flops 380928 | bytes 2539520 | tf_op jit(solution)/shard_map/mul | solution.py:105
  70.7 0.1 fusion.10
  70.8 1.0 slice.286
  71.9 0.4 copy-done.1
  72.3 0.3 slice.287
  72.5 1.5 copy.72
  74.0 2.5 %collective-permute-start.6 = (f32[3,16,32,2]{2,1,3,0:T(8,128)S(1)}, f32[3,16,32,2]{2,1,3,0:T(8,128)S(1)}, u32[]{:S(2)}, u32[]{:S(2)}) collective-permute-start(f32[3,16,32,2]{2,1,3,0:T(8,128)S(1)} %copy.72), channel_id=1, source_target_pairs={{0,1},{1,2},{2,3},{3,4},{4,5},{5,6},{6,7},{7,8},{8,9},{9,10},{10,1... | collective-permute-start | bytes 36872 | tf_op jit(solution)/shard_map/ppermute | solution.py:191
  76.5 0.3 copy.74
  76.9 4.8 %collective-permute-start.7 = (f32[3,16,32,1]{2,1,3,0:T(8,128)S(1)}, f32[3,16,32,1]{2,1,3,0:T(8,128)S(1)}, u32[]{:S(2)}, u32[]{:S(2)}) collective-permute-start(f32[3,16,32,1]{2,1,3,0:T(8,128)S(1)} %copy.74), channel_id=1, source_target_pairs={{1,0},{2,1},{3,2},{4,3},{5,4},{6,5},{7,6},{8,7},{9,8},{10,9},{11,1... | collective-permute-start | bytes 18440 | tf_op jit(solution)/shard_map/ppermute | solution.py:192
  81.6 2.0 %fusion.38 = (f32[16,32,128]{2,1,0:T(8,128)S(1)}, f32[16,32,128]{2,1,0:T(8,128)S(1)}, f32[16,32,128]{2,1,0:T(8,128)}, f32[16,32,128]{2,1,0:T(8,128)}) fusion(f32[4,20,32,2]{3,2,1,0:T(8,128)S(1)} %copy.66, f32[4,2,32,128]{3,2,1,0:T(8,128)S(1)} %collective-permute-done.1, f32[4,16,32,128]{3,2,1,0:T(8,128)S(1)} %maximum_bitcast_fusion, ...), kind=kLoop, calls=%fused_computation.66 | loop fusion | flops 1048576 | bytes 3952640 | tf_op jit(solution)/shard_map/mul | solution.py:98
  83.6 1.3 copy.75
  84.9 1.2 copy.73
  86.1 5.8 %fusion.128 = (bf16[3,16,32,128]{3,2,1,0:T(8,128)(2,1)S(1)}, f32[3,16,32,128]{3,2,1,0:T(8,128)S(1)}) fusion(f32[3,16,32,1]{3,2,1,0:T(8,128)} %copy.75, f32[3,16,32,2]{3,2,1,0:T(8,128)} %copy.73, f32[3,16,32,144]{3,2,1,0:T(8,128)S(1)} %copy-done.2, f32[3,16,31,128]{3,2,1,0:T(8,128)} %fusion.13, f32[3,18,32,130]{3,2,1,0:T(8,128)} %fusion.4, ...), kind=kLoop, calls=%fused_computation.210 | loop fusion | flops 3538944 | bytes 7727104 | tf_op jit(solution)/shard_map/convert_element_type | solution.py:198
  91.9 2.9 %collective-permute-start.9 = (bf16[3,2,32,128]{3,2,1,0:T(8,128)(2,1)S(1)}, bf16[3,2,32,128]{3,2,1,0:T(8,128)(2,1)S(1)}, u32[]{:S(2)}, u32[]{:S(2)}) collective-permute-start(bf16[3,2,32,128]{3,2,1,0:T(8,128)(2,1)S(1)} %slice.289), channel_id=1, source_target_pairs={{32,0},{64,32},{96,64},{128,96},{160,128},{192,160},{224,192},{0,2... | collective-permute-start | bytes 147464 | tf_op jit(solution)/shard_map/ppermute | solution.py:84
  94.8 4.8 %collective-permute-done.8 = bf16[3,1,32,128]{3,2,1,0:T(8,128)(2,1)S(1)} collective-permute-done((bf16[3,1,32,128]{3,2,1,0:T(8,128)(2,1)S(1)}, bf16[3,1,32,128]{3,2,1,0:T(8,128)(2,1)S(1)}, u32[]{:S(2)}, u32[]{:S(2)}) %collective-permute-start.8) | collective-permute-done | bytes 24608 | tf_op jit(solution)/shard_map/ppermute | solution.py:81
  99.7 0.4 copy.76
  100.1 7.4 %collective-permute-start.10 = (bf16[3,19,32,2]{2,3,1,0:T(2,128)(2,1)S(1)}, bf16[3,19,32,2]{2,3,1,0:T(2,128)(2,1)S(1)}, u32[]{:S(2)}, u32[]{:S(2)}) collective-permute-start(bf16[3,19,32,2]{2,3,1,0:T(2,128)(2,1)S(1)} %copy.76), channel_id=1, source_target_pairs={{1,0},{2,1},{3,2},{4,3},{5,4},{6,5},{7,6},{8,7},{9,8},{10,9},{11,1... | collective-permute-start | bytes 21896 | tf_op jit(solution)/shard_map/ppermute | solution.py:84
  107.5 0.2 slice.291
  107.7 0.5 copy.77
  108.4 4.6 %collective-permute-done.11 = bf16[3,19,32,1]{2,1,3,0:T(8,128)(2,1)S(1)} collective-permute-done((bf16[3,19,32,1]{2,1,3,0:T(8,128)(2,1)S(1)}, bf16[3,19,32,1]{2,1,3,0:T(8,128)(2,1)S(1)}, u32[]{:S(2)}, u32[]{:S(2)}) %collective-permute-start.11) | collective-permute-done | bytes 3680 | tf_op jit(solution)/shard_map/ppermute | solution.py:81
  113.0 0.5 copy.79
  113.4 0.4 copy.78
  113.9 1.3 pad_maximum_fusion.3
  115.2 11.4 %sample.1 = f32[8,3,1024]{2,1,0:T(4,128)} custom-call(bf16[3,608,144]{2,1,0:T(8,128)(2,1)} %bitcast.53, bf16[8,144,1024]{2,1,0:T(8,128)(2,1)} %get-tuple-element.7.y_ref, f32[8,24,1024]{2,1,0:T(8,128)} %get-tuple-element.8.x_ref, f32[8,32,1024]{2,1,0:T(8,128)} %get-tuple-element.9.z_ref), custom_call_target="tpu_custom_call" | custom-call | tf_op jit(solution)/shard_map/sample/pallas_call | solution.py:205
  126.6 1.0 reshape.125
  127.6 0.7 reshape.122
  128.3 11.5 %all-to-all-start.1 = ((f32[32,6,128]{2,1,0:T(8,128)}), f32[32,6,128]{2,1,0:T(8,128)S(1)}, u32[]{:S(2)}, u32[]{:S(2)}) async-start(f32[32,6,128]{2,1,0:T(8,128)} %reshape.122), calls=%async_computation.1 | async-start | bytes 262144 | tf_op jit(solution)/shard_map/all_to_all | solution.py:220
  139.8 1.3 copy.83
  141.1 10.0 %all-to-all-done.1 = f32[32,6,128]{2,1,0:T(8,128)S(1)} async-done(((f32[32,6,128]{2,1,0:T(8,128)}), f32[32,6,128]{2,1,0:T(8,128)S(1)}, u32[]{:S(2)}, u32[]{:S(2)}) %all-to-all-start.1) | async-done | bytes 98336 | tf_op jit(solution)/shard_map/all_to_all | solution.py:220
  151.1 0.8 fusion.48
  (57 shorter events, 1.1 us)
Async XLA Ops:
  2.0 6.0 %copy-start.6 = (s32[32,3,128]{2,0,1:T(8,128)S(1)}, s32[32,3,128]{2,0,1:T(8,128)}, u32[]{:S(2)}) copy-start(s32[32,3,128]{2,0,1:T(8,128)} %param.7) | copy-start | bytes 147460
  2.0 6.5 %copy-start.7 = (f32[32,3,128]{2,0,1:T(8,128)S(1)}, f32[32,3,128]{2,0,1:T(8,128)}, u32[]{:S(2)}) copy-start(f32[32,3,128]{2,0,1:T(8,128)} %param.9) | copy-start | bytes 147460
  2.0 6.4 %copy-start.8 = (f32[32,3,128]{2,0,1:T(8,128)S(1)}, f32[32,3,128]{2,0,1:T(8,128)}, u32[]{:S(2)}) copy-start(f32[32,3,128]{2,0,1:T(8,128)} %param.8) | copy-start | bytes 147460
  3.2 18.6 %collective-permute-start = (f32[4,2,32,128]{3,2,1,0:T(8,128)S(1)}, f32[4,2,32,128]{3,2,1,0:T(8,128)S(1)}, u32[]{:S(2)}, u32[]{:S(2)}) collective-permute-start(f32[4,2,32,128]{3,2,1,0:T(8,128)S(1)} %get-tuple-element.34), channel_id=1, source_target_pairs={{0,32},{32,64},{64,96},{96,128},{128,160},{160,192},{192,224},{224... | collective-permute-start | bytes 393224 | tf_op jit(solution)/shard_map/ppermute | solution.py:81
  5.4 16.5 %collective-permute-start.1 = (f32[4,2,32,128]{3,2,1,0:T(8,128)S(1)}, f32[4,2,32,128]{3,2,1,0:T(8,128)S(1)}, u32[]{:S(2)}, u32[]{:S(2)}) collective-permute-start(f32[4,2,32,128]{3,2,1,0:T(8,128)S(1)} %get-tuple-element.35), channel_id=1, source_target_pairs={{32,0},{64,32},{96,64},{128,96},{160,128},{192,160},{224,192},{0,2... | collective-permute-start | bytes 393224 | tf_op jit(solution)/shard_map/ppermute | solution.py:84
  8.4 13.5 %copy-start.9 = (s32[32]{0:T(128)}, s32[32]{0:T(128)S(1)}, u32[]{:S(2)}) copy-start(s32[32]{0:T(128)S(1)} %multiply_add_fusion.12) | copy-start | bytes 388
  9.7 33.0 %all-to-all-start = ((f32[32,18,128]{2,1,0:T(8,128)}), f32[32,18,128]{2,1,0:T(8,128)S(1)}, u32[]{:S(2)}, u32[]{:S(2)}) async-start(f32[32,18,128]{2,1,0:T(8,128)} %reshape.117), calls=%async_computation | async-start | bytes 786432 | tf_op jit(solution)/shard_map/all_to_all | solution.py:139
  25.4 4.2 %collective-permute-start.2 = (f32[4,20,32,2]{2,0,3,1:T(4,128)S(1)}, f32[4,20,32,2]{2,0,3,1:T(4,128)S(1)}, u32[]{:S(2)}, u32[]{:S(2)}) collective-permute-start(f32[4,20,32,2]{2,0,3,1:T(4,128)S(1)} %copy.64), channel_id=1, source_target_pairs={{0,1},{1,2},{2,3},{3,4},{4,5},{5,6},{6,7},{7,8},{8,9},{9,10},{10,1... | collective-permute-start | bytes 61448 | tf_op jit(solution)/shard_map/ppermute | solution.py:81
  27.7 5.1 %collective-permute-start.3 = (f32[4,20,32,2]{2,0,3,1:T(4,128)S(1)}, f32[4,20,32,2]{2,0,3,1:T(4,128)S(1)}, u32[]{:S(2)}, u32[]{:S(2)}) collective-permute-start(f32[4,20,32,2]{2,0,3,1:T(4,128)S(1)} %copy.65), channel_id=1, source_target_pairs={{1,0},{2,1},{3,2},{4,3},{5,4},{6,5},{7,6},{8,7},{9,8},{10,9},{11,1... | collective-permute-start | bytes 61448 | tf_op jit(solution)/shard_map/ppermute | solution.py:84
  37.1 1.3 copy-start
  42.8 24.6 %copy-start.4 = (f32[16,31,128]{2,1,0:T(8,128)S(1)}, f32[16,31,128]{2,1,0:T(8,128)}, u32[]{:S(2)}) copy-start(f32[16,31,128]{2,1,0:T(8,128)} %fusion.34) | copy-start | bytes 761860
  44.2 0.8 copy-start.5
  61.8 8.8 %copy-start.3 = (f32[3,608,144]{2,1,0:T(8,128)S(1)}, f32[3,608,144]{2,1,0:T(8,128)}, u32[]{:S(2)}) copy-start(f32[3,608,144]{2,1,0:T(8,128)} %get-tuple-element.6) | copy-start | bytes 3151876
  63.8 6.8 %collective-permute-start.4 = (f32[3,2,32,144]{3,2,1,0:T(8,128)S(1)}, f32[3,2,32,144]{3,2,1,0:T(8,128)S(1)}, u32[]{:S(2)}, u32[]{:S(2)}) collective-permute-start(f32[3,2,32,144]{3,2,1,0:T(8,128)S(1)} %slice.283), channel_id=1, source_target_pairs={{0,32},{32,64},{64,96},{96,128},{128,160},{160,192},{192,224},{224... | collective-permute-start | bytes 331784 | tf_op jit(solution)/shard_map/ppermute | solution.py:186
  63.8 6.8 %collective-permute-start.5 = (f32[3,1,32,144]{3,2,1,0:T(8,128)S(1)}, f32[3,1,32,144]{3,2,1,0:T(8,128)S(1)}, u32[]{:S(2)}, u32[]{:S(2)}) collective-permute-start(f32[3,1,32,144]{3,2,1,0:T(8,128)S(1)} %slice.284), channel_id=1, source_target_pairs={{32,0},{64,32},{96,64},{128,96},{160,128},{192,160},{224,192},{0,2... | collective-permute-start | bytes 165896 | tf_op jit(solution)/shard_map/ppermute | solution.py:187
  70.8 1.5 copy-start.1
  74.0 10.9 %collective-permute-start.6 = (f32[3,16,32,2]{2,1,3,0:T(8,128)S(1)}, f32[3,16,32,2]{2,1,3,0:T(8,128)S(1)}, u32[]{:S(2)}, u32[]{:S(2)}) collective-permute-start(f32[3,16,32,2]{2,1,3,0:T(8,128)S(1)} %copy.72), channel_id=1, source_target_pairs={{0,1},{1,2},{2,3},{3,4},{4,5},{5,6},{6,7},{7,8},{8,9},{9,10},{10,1... | collective-permute-start | bytes 36872 | tf_op jit(solution)/shard_map/ppermute | solution.py:191
  76.9 6.8 %collective-permute-start.7 = (f32[3,16,32,1]{2,1,3,0:T(8,128)S(1)}, f32[3,16,32,1]{2,1,3,0:T(8,128)S(1)}, u32[]{:S(2)}, u32[]{:S(2)}) collective-permute-start(f32[3,16,32,1]{2,1,3,0:T(8,128)S(1)} %copy.74), channel_id=1, source_target_pairs={{1,0},{2,1},{3,2},{4,3},{5,4},{6,5},{7,6},{8,7},{9,8},{10,9},{11,1... | collective-permute-start | bytes 18440 | tf_op jit(solution)/shard_map/ppermute | solution.py:192
  83.6 2.5 %copy-start.2 = (f32[3,16,32,144]{3,2,1,0:T(8,128)S(1)}, f32[3,16,32,144]{3,2,1,0:T(8,128)}, u32[]{:S(2)}) copy-start(f32[3,16,32,144]{3,2,1,0:T(8,128)} %copy-done.1) | copy-start | bytes 2654212
  91.9 7.7 %collective-permute-start.9 = (bf16[3,2,32,128]{3,2,1,0:T(8,128)(2,1)S(1)}, bf16[3,2,32,128]{3,2,1,0:T(8,128)(2,1)S(1)}, u32[]{:S(2)}, u32[]{:S(2)}) collective-permute-start(bf16[3,2,32,128]{3,2,1,0:T(8,128)(2,1)S(1)} %slice.289), channel_id=1, source_target_pairs={{32,0},{64,32},{96,64},{128,96},{160,128},{192,160},{224,192},{0,2... | collective-permute-start | bytes 147464 | tf_op jit(solution)/shard_map/ppermute | solution.py:84
  94.8 4.8 %collective-permute-start.8 = (bf16[3,1,32,128]{3,2,1,0:T(8,128)(2,1)S(1)}, bf16[3,1,32,128]{3,2,1,0:T(8,128)(2,1)S(1)}, u32[]{:S(2)}, u32[]{:S(2)}) collective-permute-start(bf16[3,1,32,128]{3,2,1,0:T(8,128)(2,1)S(1)} %slice.288), channel_id=1, source_target_pairs={{0,32},{32,64},{64,96},{96,128},{128,160},{160,192},{192,224},{224... | collective-permute-start | bytes 73736 | tf_op jit(solution)/shard_map/ppermute | solution.py:81
  100.1 13.4 %collective-permute-start.10 = (bf16[3,19,32,2]{2,3,1,0:T(2,128)(2,1)S(1)}, bf16[3,19,32,2]{2,3,1,0:T(2,128)(2,1)S(1)}, u32[]{:S(2)}, u32[]{:S(2)}) collective-permute-start(bf16[3,19,32,2]{2,3,1,0:T(2,128)(2,1)S(1)} %copy.76), channel_id=1, source_target_pairs={{1,0},{2,1},{3,2},{4,3},{5,4},{6,5},{7,6},{8,7},{9,8},{10,9},{11,1... | collective-permute-start | bytes 21896 | tf_op jit(solution)/shard_map/ppermute | solution.py:84
  108.2 4.8 %collective-permute-start.11 = (bf16[3,19,32,1]{2,1,3,0:T(8,128)(2,1)S(1)}, bf16[3,19,32,1]{2,1,3,0:T(8,128)(2,1)S(1)}, u32[]{:S(2)}, u32[]{:S(2)}) collective-permute-start(bf16[3,19,32,1]{2,1,3,0:T(8,128)(2,1)S(1)} %copy.77), channel_id=1, source_target_pairs={{0,1},{1,2},{2,3},{3,4},{4,5},{5,6},{6,7},{7,8},{8,9},{9,10},{10,1... | collective-permute-start | bytes 10952 | tf_op jit(solution)/shard_map/ppermute | solution.py:81
  126.5 24.6 %copy-start.10 = (s32[32]{0:T(128)S(1)}, s32[32]{0:T(128)}, u32[]{:S(2)}) copy-start(s32[32]{0:T(128)} %copy-done.9) | copy-start | bytes 388
  128.3 22.8 %all-to-all-start.1 = ((f32[32,6,128]{2,1,0:T(8,128)}), f32[32,6,128]{2,1,0:T(8,128)S(1)}, u32[]{:S(2)}, u32[]{:S(2)}) async-start(f32[32,6,128]{2,1,0:T(8,128)} %reshape.122), calls=%async_computation.1 | async-start | bytes 262144 | tf_op jit(solution)/shard_map/all_to_all | solution.py:220

commit v2 on v1

--- a/solution.py
+++ b/solution.py
@@ -1,3 +1,5 @@
+import functools
+
 import jax
 import jax.numpy as jnp
 from jax import lax
@@ -36,9 +38,12 @@
     return matrix
 
 
-def spread_kernel(cells, weights, forces, total, y_out, x_out, z_out, lifted):
+def spread_kernel(
+    cells, weights, forces, core, above, below, y_out, x_out, z_out, lifted, total
+):
     depth = z_out.shape[1]
     markers = cells.shape[2]
+    rows = lifted.shape[0]
 
     @pl.when(pl.program_id(0) == 0)
     def _():
@@ -59,55 +64,226 @@
                 lifted[x * depth : (x + 1) * depth, lanes] = (
                     scaled * x_out[0, x : x + 1, lanes]
                 ).astype(jnp.bfloat16)
-        total[comp] += lax.dot_general(
+        total[comp, 0:rows, 0:YR] += lax.dot_general(
             lifted[...], y_out[0], (((1,), (1,)), ((), ())), preferred_element_type=jnp.float32
         )
+
+    @pl.when(pl.program_id(0) == pl.num_programs(0) - 1)
+    def _():
+        for comp in range(3):
+            core[comp] = total[comp, :, 0:128]
+            for tile in range(5):
+                turned = total[comp, tile * 128 : (tile + 1) * 128, 128:256].T
+                above[comp, tile] = turned[0:8]
+                below[comp, tile] = turned[8:16]
 
 
 def sample_kernel(field, y_ref, x_ref, z_ref, out):
     depth = z_ref.shape[1]
     for comp in range(3):
-        along_y = jnp.dot(field[comp], y_ref[0], preferred_element_type=jnp.float32)
+        along_y = jnp.dot(
+            field[comp, 0 : XR * depth, 0:YR], y_ref[0], preferred_element_type=jnp.float32
+        )
         column = along_y[0:depth] * x_ref[0, 0:1, :]
         for x in range(1, XR):
             column = column + along_y[x * depth : (x + 1) * depth] * x_ref[0, x : x + 1, :]
         out[0, comp : comp + 1, :] = jnp.sum(column * z_ref[0], axis=0, keepdims=True)
 
 
-def exchange(array, axis, dim, low_width, high_width):
-    count, length = lax.axis_size(axis), array.shape[dim]
-    up = [(i, (i + 1) % count) for i in range(count)]
-    down = [(j, i) for i, j in up]
-    before = lax.ppermute(
-        lax.slice_in_dim(array, length - low_width, length, axis=dim), axis, up
-    )
-    after = lax.ppermute(lax.slice_in_dim(array, 0, high_width, axis=dim), axis, down)
-    return before, after
-
-
-def padded(array, axis, dim, width):
-    before, after = exchange(array, axis, dim, width, width)
-    return jnp.concatenate([before, array, after], axis=dim)
-
-
-def relax(field, visc):
-    center_field = field[:, 1:-1, :, 1:-1]
-    center_visc = visc[:, 1:-1, :, 1:-1]
-
-    def face(neighbor_field, neighbor_visc):
-        return 0.5 * (center_visc + neighbor_visc) * (neighbor_field - center_field)
-
-    total = face(field[:, :-2, :, 1:-1], visc[:, :-2, :, 1:-1])
-    total = total + face(field[:, 2:, :, 1:-1], visc[:, 2:, :, 1:-1])
-    total = total + face(field[:, 1:-1, :, :-2], visc[:, 1:-1, :, :-2])
-    total = total + face(field[:, 1:-1, :, 2:], visc[:, 1:-1, :, 2:])
-    vertical = center_field[:, :, 1:] - center_field[:, :, :-1]
-    vertical = 0.5 * (center_visc[:, :, 1:] + center_visc[:, :, :-1]) * vertical
-    zeros_layer = jnp.zeros_like(vertical[:, :, :1])
-    z_term = jnp.concatenate([vertical, zeros_layer], axis=2) - jnp.concatenate(
-        [zeros_layer, vertical], axis=2
-    )
-    return center_field + (total + z_term)
+def settle_kernel(
+    count_x, count_y, stacked, core, above, below,
+    final, field,
+    wide, first, force, rim, from_low_y, from_high_y, from_low_x, from_high_x,
+    to_high, to_low, ghost_low, ghost_high, rim_up, rim_down, rim_low, rim_high,
+    send_sems, recv_sems,
+):
+    me_x, me_y = lax.axis_index("gx"), lax.axis_index("gy")
+    up_x = (lax.rem(me_x + 1, count_x), me_y)
+    down_x = (lax.rem(me_x + count_x - 1, count_x), me_y)
+    up_y = (me_x, lax.rem(me_y + 1, count_y))
+    down_y = (me_x, lax.rem(me_y + count_y - 1, count_y))
+
+    barrier = pltpu.get_barrier_semaphore()
+    for device in (up_x, down_x, up_y, down_y):
+        pl.semaphore_signal(barrier, inc=1, device_id=device, device_id_type=pl.DeviceIdType.MESH)
+    pl.semaphore_wait(barrier, 4)
+
+    def send(number, source, target, device):
+        copy = pltpu.make_async_remote_copy(
+            src_ref=source,
+            dst_ref=target,
+            send_sem=send_sems.at[number],
+            recv_sem=recv_sems.at[number],
+            device_id=device,
+            device_id_type=pl.DeviceIdType.MESH,
+        )
+        copy.start()
+        return copy
+
+    def tiles(comps, body):
+        def step(index, carry):
+            body(index // 5, lax.rem(index, 5))
+            return carry
+
+        lax.fori_loop(0, comps * 5, step, 0)
+
+    x_up = send(0, stacked.at[:, 14:16], wide.at[:, 0:2, :, 0:128], up_x)
+    x_down = send(1, stacked.at[:, 0:2], wide.at[:, 18:20, :, 0:128], down_x)
+    y_up = send(2, above, from_low_y, up_y)
+    y_down = send(3, below, from_high_y, down_y)
+
+    wide[:, 2:18, :, 0:128] = stacked[...]
+    rim[:, 19:20] = jnp.zeros_like(rim[:, 19:20])
+    x_up.wait()
+    x_down.wait()
+
+    def turn_wide(comp, tile):
+        turned = wide[comp, pl.ds(4 * tile, 4), :, 0:128].reshape(128, 128).T
+        to_low[comp, tile] = turned[0:8]
+        to_high[comp, tile] = turned[120:128]
+
+    tiles(4, turn_wide)
+    wide_up = send(4, to_high, ghost_low, up_y)
+    wide_down = send(5, to_low, ghost_high, down_y)
+    y_up.wait()
+    y_down.wait()
+
+    def add_force(comp, tile):
+        middle = jnp.zeros((112, 128), jnp.float32)
+        turned = jnp.concatenate(
+            [from_low_y[comp, tile], middle, from_high_y[comp, tile]], axis=0
+        ).T
+        part = pl.ds(4 * tile, 4)
+        force[comp, part] = core[comp, part] + turned.reshape(4, 32, 128)
+
+    tiles(3, add_force)
+    force_up = send(6, force.at[:, 17:19], from_low_x, up_x)
+    force_down = send(7, force.at[:, 0:1], from_high_x, down_x)
+    wide_up.wait()
+    wide_down.wait()
+
+    def fill_wide(comp, tile):
+        middle = jnp.zeros((112, 128), jnp.float32)
+        turned = jnp.concatenate(
+            [ghost_high[comp, tile], middle, ghost_low[comp, tile]], axis=0
+        ).T
+        wide[comp, pl.ds(4 * tile, 4), :, 128:256] = turned.reshape(4, 32, 128)
+
+    tiles(4, fill_wide)
+
+    height = lax.broadcasted_iota(jnp.int32, (32, 256), 0)
+
+    def relaxed(source, x, visc_x, store):
+        visc = wide[3, visc_x]
+        low_x = 0.5 * (visc + wide[3, visc_x - 1])
+        high_x = 0.5 * (visc + wide[3, visc_x + 1])
+        low_y = 0.5 * (visc + pltpu.roll(visc, 1, 1))
+        high_y = 0.5 * (visc + pltpu.roll(visc, 255, 1))
+        low_z = jnp.where(height > 0, 0.5 * (visc + pltpu.roll(visc, 1, 0)), 0.0)
+        high_z = jnp.where(height < 31, 0.5 * (visc + pltpu.roll(visc, 31, 0)), 0.0)
+        for comp in range(3):
+            here = source[comp, x]
+            total = low_x * (source[comp, x - 1] - here)
+            total = total + high_x * (source[comp, x + 1] - here)
+            total = total + low_y * (pltpu.roll(here, 1, 1) - here)
+            total = total + high_y * (pltpu.roll(here, 255, 1) - here)
+            total = total + low_z * (pltpu.roll(here, 1, 0) - here)
+            total = total + high_z * (pltpu.roll(here, 31, 0) - here)
+            store(comp, here + total)
+
+    def first_step(x, carry):
+        def store(comp, value):
+            first[comp, x - 1] = value
+
+        relaxed(wide, x, x, store)
+        return carry
+
+    lax.fori_loop(1, 19, first_step, 0)
+
+    force_up.wait()
+    force_down.wait()
+    force[:, 1:3] = force[:, 1:3] + from_low_x[...]
+    force[:, 16:17] = force[:, 16:17] + from_high_x[...]
+
+    def second_step(x, carry):
+        def store(comp, value):
+            total = value[:, 0:128] + force[comp, x]
+            final[comp, x - 1] = total
+            rim[comp, x] = total.astype(jnp.bfloat16)
+
+        relaxed(first, x, x + 1, store)
+        return carry
+
+    lax.fori_loop(1, 17, second_step, 0)
+
+    rim_x_up = send(8, rim.at[:, 16:17], rim.at[:, 0:1], up_x)
+    rim_x_down = send(9, rim.at[:, 1:3], rim.at[:, 17:19], down_x)
+    rim_x_up.wait()
+    rim_x_down.wait()
+
+    def turn_rim(comp, tile):
+        part = pl.ds(4 * tile, 4)
+        rows = rim[comp, part]
+        field[comp, part, :, 0:128] = rows
+        turned = rows.astype(jnp.float32).reshape(128, 128).T
+        rim_down[comp, tile] = turned[0:8]
+        rim_up[comp, tile] = turned[120:128]
+
+    tiles(3, turn_rim)
+    rim_y_up = send(10, rim_up, rim_low, up_y)
+    rim_y_down = send(11, rim_down, rim_high, down_y)
+    rim_y_up.wait()
+    rim_y_down.wait()
+
+    def fill_field(comp, tile):
+        rest = jnp.zeros((112, 128), jnp.float32)
+        turned = jnp.concatenate([rim_high[comp, tile], rim_low[comp, tile], rest], axis=0).T
+        field[comp, pl.ds(4 * tile, 4), :, 128:256] = turned.reshape(4, 32, 128).astype(
+            jnp.bfloat16
+        )
+
+    tiles(3, fill_field)
+
+
+def settle(stacked, core, above, below):
+    vmem = pl.BlockSpec(memory_space=pltpu.VMEM)
+
+    def ghosts(comps):
+        return pltpu.VMEM((comps, 5, 8, 128), jnp.float32)
+
+    return pl.pallas_call(
+        functools.partial(settle_kernel, lax.axis_size("gx"), lax.axis_size("gy")),
+        in_specs=[vmem] * 4,
+        out_specs=[vmem] * 2,
+        out_shape=[
+            jax.ShapeDtypeStruct((3, 16, 32, 128), jnp.float32),
+            jax.ShapeDtypeStruct((3, 20, 32, 256), jnp.bfloat16),
+        ],
+        scratch_shapes=[
+            pltpu.VMEM((4, 20, 32, 256), jnp.float32),
+            pltpu.VMEM((3, 18, 32, 256), jnp.float32),
+            pltpu.VMEM((3, 20, 32, 128), jnp.float32),
+            pltpu.VMEM((3, 20, 32, 128), jnp.bfloat16),
+            ghosts(3),
+            ghosts(3),
+            pltpu.VMEM((3, 2, 32, 128), jnp.float32),
+            pltpu.VMEM((3, 1, 32, 128), jnp.float32),
+            ghosts(4),
+            ghosts(4),
+            ghosts(4),
+            ghosts(4),
+            ghosts(3),
+            ghosts(3),
+            ghosts(3),
+            ghosts(3),
+            pltpu.SemaphoreType.DMA((12,)),
+            pltpu.SemaphoreType.DMA((12,)),
+        ],
+        compiler_params=pltpu.CompilerParams(
+            collective_id=0, has_side_effects=True, vmem_limit_bytes=40 * 2**20
+        ),
+        name="settle",
+    )(stacked, core, above, below)
 
 
 def body(velocity, viscosity, marker_cells, marker_offset, marker_force):
@@ -146,7 +322,7 @@
 
     rows = XR * depth
     lanes = GROUP * markers
-    total, y_matrix, x_matrix, z_matrix = pl.pallas_call(
+    core, above, below, y_matrix, x_matrix, z_matrix = pl.pallas_call(
         spread_kernel,
         grid=(steps,),
         in_specs=[
@@ -155,58 +331,38 @@
             pl.BlockSpec((3, GROUP, markers), lambda g: (0, g, 0)),
         ],
         out_specs=[
-            pl.BlockSpec((3, rows, YR), lambda g: (0, 0, 0)),
+            pl.BlockSpec((3, 640, 128), lambda g: (0, 0, 0)),
+            pl.BlockSpec((3, 5, 8, 128), lambda g: (0, 0, 0, 0)),
+            pl.BlockSpec((3, 5, 8, 128), lambda g: (0, 0, 0, 0)),
             pl.BlockSpec((1, YR, lanes), lambda g: (g, 0, 0)),
             pl.BlockSpec((1, 24, lanes), lambda g: (g, 0, 0)),
             pl.BlockSpec((1, depth, lanes), lambda g: (g, 0, 0)),
         ],
         out_shape=[
-            jax.ShapeDtypeStruct((3, rows, YR), jnp.float32),
+            jax.ShapeDtypeStruct((3, 640, 128), jnp.float32),
+            jax.ShapeDtypeStruct((3, 5, 8, 128), jnp.float32),
+            jax.ShapeDtypeStruct((3, 5, 8, 128), jnp.float32),
             jax.ShapeDtypeStruct((steps, YR, lanes), jnp.bfloat16),
             jax.ShapeDtypeStruct((steps, 24, lanes), jnp.float32),
             jax.ShapeDtypeStruct((steps, depth, lanes), jnp.float32),
         ],
-        scratch_shapes=[pltpu.VMEM((rows, lanes), jnp.bfloat16)],
+        scratch_shapes=[
+            pltpu.VMEM((rows, lanes), jnp.bfloat16),
+            pltpu.VMEM((3, 640, 256), jnp.float32),
+        ],
         name="spread",
     )(cells, weights, forces)
 
     stacked = jnp.concatenate([velocity, viscosity[None]], axis=0)
     stacked = jnp.swapaxes(stacked, 1, 2)
-    stacked = padded(padded(stacked, "gx", 1, 2), "gy", 3, 2)
-    visc = stacked[3:4]
-    first = relax(stacked[0:3], visc)
-    second = relax(first, visc[:, 1:-1, :, 1:-1])
-
-    total = total.reshape(3, XR, depth, YR)
-    count_x, count_y = lax.axis_size("gx"), lax.axis_size("gy")
-    up_x = [(i, (i + 1) % count_x) for i in range(count_x)]
-    down_x = [(j, i) for i, j in up_x]
-    up_y = [(i, (i + 1) % count_y) for i in range(count_y)]
-    down_y = [(j, i) for i, j in up_y]
-    from_low = lax.ppermute(total[:, width_x + 1 :], "gx", up_x)
-    from_high = lax.ppermute(total[:, 0:1], "gx", down_x)
-    core = total[:, 1 : width_x + 1]
-    core = core + jnp.pad(from_low, ((0, 0), (0, width_x - 2), (0, 0), (0, 0)))
-    core = core + jnp.pad(from_high, ((0, 0), (width_x - 1, 0), (0, 0), (0, 0)))
-    from_low = lax.ppermute(core[..., width_y : width_y + 2], "gy", up_y)
-    from_high = lax.ppermute(core[..., YR - 1 :], "gy", down_y)
-    force = core[..., :width_y]
-    force = force + jnp.pad(from_low, ((0, 0), (0, 0), (0, 0), (0, width_y - 2)))
-    force = force + jnp.pad(from_high, ((0, 0), (0, 0), (0, 0), (width_y - 1, 0)))
-    final = second + force
-
-    rounded = final.astype(jnp.bfloat16)
-    before, after = exchange(rounded, "gx", 1, 1, 2)
-    rounded = jnp.concatenate([before, rounded, after], axis=1)
-    before, after = exchange(rounded, "gy", 3, 1, 2)
-    middle = jnp.zeros((3, XR, depth, YR - width_y - 3), jnp.bfloat16)
-    field = jnp.concatenate([rounded, after, middle, before], axis=3).reshape(3, rows, YR)
+    final, field = settle(stacked, core.reshape(3, 20, depth, width_y), above, below)
+    field = field.reshape(3, 640, 256)
 
     sampled = pl.pallas_call(
         sample_kernel,
         grid=(steps,),
         in_specs=[
-            pl.BlockSpec((3, rows, YR), lambda g: (0, 0, 0)),
+            pl.BlockSpec((3, 640, 256), lambda g: (0, 0, 0)),
             pl.BlockSpec((1, YR, lanes), lambda g: (g, 0, 0)),
             pl.BlockSpec((1, 24, lanes), lambda g: (g, 0, 0)),
             pl.BlockSpec((1, depth, lanes), lambda g: (g, 0, 0)),

time: 153 us -> 122 us (0.80)
  Pallas kernels: 28.3 us -> 59.9 us
  starting transfers between devices: 51.6 us -> 21.3 us
  other arithmetic: 23 us -> 2.3 us
  local copies, waits for them, and re-layouts: 23.9 us -> 10.7 us
    pallas_call x1 -> x2, Pallas kernels: 11.4 us -> 42.8 us  [the longest x1 31.4 us: settle(): pl.pallas_call(functools.partial(settle_kernel, lax.axis_size('gx'), lax....]
    ppermute x12 -> x0, starting transfers between devices: 28 us -> none  [the longest x4 13.3 us: exchange(): lax.ppermute(lax.slice_in_dim(array, 0, high_width, axis=dim), axis, down)]
    all_to_all x1, waiting for transfers between devices: 0.01 us -> 14.6 us  [body(): received = lax.all_to_all(sent, 'gy', 0, 0, tiled=True)]
    ppermute x12 -> x0, waiting for transfers between devices: 12.9 us -> none  [the longest x4 10.4 us: exchange(): lax.ppermute(lax.slice_in_dim(array, length - low_width, length, axis=dim...]
    slice x15 -> x0, local copies, waits for them, and re-layouts: 10.2 us -> none  [the longest x6 4.12 us: exchange(): lax.slice_in_dim(array, length - low_width, length, axis=dim)]
    mul x6 -> x0, other arithmetic: 8.04 us -> none  [the longest x4 5.35 us: relax(): vertical = 0.5 * (center_visc[:, :, 1:] + center_visc[:, :, :-1]) * vertical]
    convert_element_type x1 -> x0, other arithmetic: 5.76 us -> none  [body(): rounded = final.astype(jnp.bfloat16)]
    ppermute x6 -> x0, local copies, waits for them, and re-layouts: 5.57 us -> none  [the longest x2 2.08 us: exchange(): lax.ppermute(lax.slice_in_dim(array, 0, high_width, axis=dim), axis, down)]
  transfers between devices with their start and end apart: 14 -> 2, of which waited for: 5 -> 2; matrix products, arithmetic and copies ran while one was open for 17% -> 2% of each run, Pallas kernels for 0% -> 0%
where the time goes in v2:
time: 122 us; the launch traced here: 121 us
  Pallas kernels  59.9 us (49%)
  waiting for transfers between devices  23.9 us (20%)
  starting transfers between devices  21.3 us (17%)
  local copies, waits for them, and re-layouts  10.7 us (9%)
  other arithmetic  2.3 us (2%)
  matrix products  2.06 us (2%)
    pallas_call x1, Pallas kernels, settle(): pl.pallas_call(functools.partial(settle_kernel, lax.axis_size('gx'), lax....  31.4 us
    pallas_call x1, Pallas kernels, body(): pl.pallas_call(spread_kernel, grid=(steps,), in_specs=[pl.BlockSpec((3, G...  17.1 us
    all_to_all x1, waiting for transfers between devices, body(): received = lax.all_to_all(sent, 'gy', 0, 0, tiled=True)  14.6 us
    all_to_all x1, starting transfers between devices, body(): received = lax.all_to_all(sent, 'gy', 0, 0, tiled=True)  12.8 us
    pallas_call x1, Pallas kernels, body(): pl.pallas_call(sample_kernel, grid=(steps,), in_specs=[pl.BlockSpec((3, 6...  11.4 us
    all_to_all x1, waiting for transfers between devices, body(): lax.all_to_all(sampled, 'gy', 0, 0, tiled=True).reshape(slots, -1)  9.31 us
    all_to_all x1, starting transfers between devices, body(): lax.all_to_all(sampled, 'gy', 0, 0, tiled=True).reshape(slots, -1)  8.56 us
    unnamed x15, local copies, waits for them, and re-layouts  7.17 us
  transfers between devices with their start and end apart: 2, of which 2 were waited for; matrix products, arithmetic and copies ran while one was open for 2% of the time, Pallas kernels for 0%

profile of v2, /device:TPU:1, one launch (start us, length us, event | category | flops | bytes accessed | tf_op | source)
XLA Modules:
  0.0 121.1 jit_solution(12131028163070525929)
XLA Ops:
  0.6 0.0 copy-start.4
  0.6 0.9 slice_reduce_fusion
  1.6 0.2 select_reduce_fusion
  1.8 0.8 slice_subtract_fusion.1
  2.6 1.2 %fusion = f32[64,1152]{1,0:T(8,128)S(1)} fusion(s32[32]{0:T(128)S(1)} %multiply_add_fusion.12, f32[32,3,128]{2,0,1:T(8,128)} %param.9, f32[32,3,128]{2,0,1:T(8,128)} %param.8, f32[32,3,128]{2,0,1:T(8,128)S(1)} %add_convert_fusion), kind=kOutput, calls=%fused_computation.3 | convolution fusion | flops 28387328 | bytes 442496 | tf_op jit(solution)/shard_map/dot_general | solution.py:313
  3.8 0.8 reshape.117
  4.7 12.8 %all-to-all-start = ((f32[32,18,128]{2,1,0:T(8,128)}), f32[32,18,128]{2,1,0:T(8,128)S(1)}, u32[]{:S(2)}, u32[]{:S(2)}) async-start(f32[32,18,128]{2,1,0:T(8,128)} %reshape.117), calls=%async_computation | async-start | bytes 786432 | tf_op jit(solution)/shard_map/all_to_all | solution.py:315
  17.4 1.0 copy.41
  18.5 0.0 copy-done.4
  18.5 0.3 copy.19
  18.7 0.1 maximum_bitcast_fusion.stacked
  18.8 14.6 %all-to-all-done = f32[32,18,128]{2,1,0:T(8,128)S(1)} async-done(((f32[32,18,128]{2,1,0:T(8,128)}), f32[32,18,128]{2,1,0:T(8,128)S(1)}, u32[]{:S(2)}, u32[]{:S(2)}) %all-to-all-start) | async-done | bytes 294944 | tf_op jit(solution)/shard_map/all_to_all | solution.py:315
  33.5 0.1 copy.40
  33.6 0.7 fusion.83
  34.9 0.0 copy-start.5
  34.9 0.7 copy-done.5
  35.6 17.1 %spread.1 = (f32[3,640,128]{2,1,0:T(8,128)}, f32[3,5,8,128]{3,2,1,0:T(8,128)}, f32[3,5,8,128]{3,2,1,0:T(8,128)}, bf16[8,144,1024]{2,1,0:T(8,128)(2,1)}, f32[8,24,1024]{2,1,0:T(8,128)}, /*index=5*/f32[8,32,1024]{2,1,0:T(8,128)}) custom-call(s32[3,64,128]{2,1,0:T(8,128)} %get-tuple-element.27.cells, f32[12,64,128]{2,1,0:T(8,128)} %copy-done.5, ...), custom_call_target="tpu_custom_call" | custom-call | tf_op jit(solution)/shard_map/spread/pallas_call | solution.py:325
  52.7 0.0 copy-start
  52.7 1.2 copy-done
  53.9 0.0 copy-start.2
  53.9 0.8 copy-done.2
  54.8 0.0 copy-start.3
  54.8 0.8 copy-done.3
  55.6 31.4 %settle.1 = (f32[3,16,32,128]{3,2,1,0:T(8,128)S(1)}, bf16[3,20,32,256]{3,2,1,0:T(8,128)(2,1)S(1)}) custom-call(f32[4,16,32,128]{3,2,1,0:T(8,128)S(1)} %maximum_bitcast_fusion.stacked, f32[3,20,32,128]{3,2,1,0:T(8,128)S(1)} %bitcast.31, f32[3,5,8,128]{3,2,1,0:T(8,128)S(1)} %copy-done.2, f32[3,5,8,128]{3,2,1,0:T(8,128)S(1)} %copy-done.3), custom_call_target="tpu_custom_call" | custom-call | tf_op jit(solution)/shard_map/settle/pallas_call | solution.py:254
  87.0 0.0 copy-start.1
  87.0 0.9 copy-done.1
  87.9 11.4 %sample.1 = f32[8,3,1024]{2,1,0:T(4,128)} custom-call(bf16[3,640,256]{2,1,0:T(8,128)(2,1)} %bitcast.32, bf16[8,144,1024]{2,1,0:T(8,128)(2,1)} %get-tuple-element.15.y_ref, f32[8,24,1024]{2,1,0:T(8,128)} %get-tuple-element.16.x_ref, f32[8,32,1024]{2,1,0:T(8,128)} %get-tuple-element.17.z_ref), custom_call_target="tpu_custom_call" | custom-call | tf_op jit(solution)/shard_map/sample/pallas_call | solution.py:361
  99.3 1.0 reshape.125
  100.3 0.7 reshape.122
  101.0 8.6 %all-to-all-start.1 = ((f32[32,6,128]{2,1,0:T(8,128)}), f32[32,6,128]{2,1,0:T(8,128)S(1)}, u32[]{:S(2)}, u32[]{:S(2)}) async-start(f32[32,6,128]{2,1,0:T(8,128)} %reshape.122), calls=%async_computation.1 | async-start | bytes 262144 | tf_op jit(solution)/shard_map/all_to_all | solution.py:376
  109.6 1.3 %copy.25 = f32[3,32,16,128]{3,2,1,0:T(8,128)} copy(f32[3,32,16,128]{3,1,2,0:T(8,128)S(1)} %bitcast.33) | data formatting | bytes 1572864
  110.9 9.3 %all-to-all-done.1 = f32[32,6,128]{2,1,0:T(8,128)S(1)} async-done(((f32[32,6,128]{2,1,0:T(8,128)}), f32[32,6,128]{2,1,0:T(8,128)S(1)}, u32[]{:S(2)}, u32[]{:S(2)}) %all-to-all-start.1) | async-done | bytes 98336 | tf_op jit(solution)/shard_map/all_to_all | solution.py:376
  120.2 0.8 fusion.3
  (18 shorter events, 0.6 us)
Async XLA Ops:
  0.6 17.8 %copy-start.4 = (f32[3,32,16,128]{3,2,1,0:T(8,128)S(1)}, f32[3,32,16,128]{3,2,1,0:T(8,128)}, u32[]{:S(2)}) copy-start(f32[3,32,16,128]{3,2,1,0:T(8,128)} %param.5) | copy-start | bytes 2359300
  4.7 28.8 %all-to-all-start = ((f32[32,18,128]{2,1,0:T(8,128)}), f32[32,18,128]{2,1,0:T(8,128)S(1)}, u32[]{:S(2)}, u32[]{:S(2)}) async-start(f32[32,18,128]{2,1,0:T(8,128)} %reshape.117), calls=%async_computation | async-start | bytes 786432 | tf_op jit(solution)/shard_map/all_to_all | solution.py:315
  34.9 0.7 copy-start.5
  52.7 1.2 copy-start
  53.9 0.8 copy-start.2
  54.8 0.8 copy-start.3
  87.0 0.9 copy-start.1
  101.0 19.2 %all-to-all-start.1 = ((f32[32,6,128]{2,1,0:T(8,128)}), f32[32,6,128]{2,1,0:T(8,128)S(1)}, u32[]{:S(2)}, u32[]{:S(2)}) async-start(f32[32,6,128]{2,1,0:T(8,128)} %reshape.122), calls=%async_computation.1 | async-start | bytes 262144 | tf_op jit(solution)/shard_map/all_to_all | solution.py:376

commit v3 on v2

--- a/solution.py
+++ b/solution.py
@@ -42,8 +42,10 @@
     cells, weights, forces, core, above, below, y_out, x_out, z_out, lifted, total
 ):
     depth = z_out.shape[1]
-    markers = cells.shape[2]
+    markers = cells.shape[3]
     rows = lifted.shape[0]
+    step = pl.program_id(0)
+    cells, weights, forces = cells.at[:, step], weights.at[:, step], forces.at[:, step]
 
     @pl.when(pl.program_id(0) == 0)
     def _():
@@ -87,27 +89,32 @@
         column = along_y[0:depth] * x_ref[0, 0:1, :]
         for x in range(1, XR):
             column = column + along_y[x * depth : (x + 1) * depth] * x_ref[0, x : x + 1, :]
-        out[0, comp : comp + 1, :] = jnp.sum(column * z_ref[0], axis=0, keepdims=True)
-
-
-def settle_kernel(
-    count_x, count_y, stacked, core, above, below,
-    final, field,
-    wide, first, force, rim, from_low_y, from_high_y, from_low_x, from_high_x,
-    to_high, to_low, ghost_low, ghost_high, rim_up, rim_down, rim_low, rim_high,
-    send_sems, recv_sems,
-):
+        result = jnp.sum(column * z_ref[0], axis=0, keepdims=True)
+        for slot in range(GROUP):
+            row = (slot % CAP) * 3 + comp
+            out[slot // CAP, row : row + 1, :] = result[:, slot * 128 : (slot + 1) * 128]
+
+
+MESH = pl.DeviceIdType.MESH
+
+
+def neighbours(count_x, count_y):
     me_x, me_y = lax.axis_index("gx"), lax.axis_index("gy")
     up_x = (lax.rem(me_x + 1, count_x), me_y)
     down_x = (lax.rem(me_x + count_x - 1, count_x), me_y)
     up_y = (me_x, lax.rem(me_y + 1, count_y))
     down_y = (me_x, lax.rem(me_y + count_y - 1, count_y))
-
+    return up_x, down_x, up_y, down_y
+
+
+def greet(devices):
     barrier = pltpu.get_barrier_semaphore()
-    for device in (up_x, down_x, up_y, down_y):
-        pl.semaphore_signal(barrier, inc=1, device_id=device, device_id_type=pl.DeviceIdType.MESH)
-    pl.semaphore_wait(barrier, 4)
-
+    for device in devices:
+        pl.semaphore_signal(barrier, inc=1, device_id=device, device_id_type=MESH)
+    pl.semaphore_wait(barrier, len(devices))
+
+
+def sender(send_sems, recv_sems):
     def send(number, source, target, device):
         copy = pltpu.make_async_remote_copy(
             src_ref=source,
@@ -115,25 +122,32 @@
             send_sem=send_sems.at[number],
             recv_sem=recv_sems.at[number],
             device_id=device,
-            device_id_type=pl.DeviceIdType.MESH,
+            device_id_type=MESH,
         )
         copy.start()
         return copy
 
-    def tiles(comps, body):
-        def step(index, carry):
-            body(index // 5, lax.rem(index, 5))
-            return carry
-
-        lax.fori_loop(0, comps * 5, step, 0)
-
+    return send
+
+
+def tiles(comps, body):
+    def step(index, carry):
+        body(index // 5, lax.rem(index, 5))
+        return carry
+
+    lax.fori_loop(0, comps * 5, step, 0)
+
+
+def flow_kernel(
+    count_x, count_y, stacked, second, wide, first, to_high, to_low, ghost_low, ghost_high,
+    send_sems, recv_sems,
+):
+    up_x, down_x, up_y, down_y = neighbours(count_x, count_y)
+    greet((up_x, down_x, up_y, down_y))
+    send = sender(send_sems, recv_sems)
     x_up = send(0, stacked.at[:, 14:16], wide.at[:, 0:2, :, 0:128], up_x)
     x_down = send(1, stacked.at[:, 0:2], wide.at[:, 18:20, :, 0:128], down_x)
-    y_up = send(2, above, from_low_y, up_y)
-    y_down = send(3, below, from_high_y, down_y)
-
     wide[:, 2:18, :, 0:128] = stacked[...]
-    rim[:, 19:20] = jnp.zeros_like(rim[:, 19:20])
     x_up.wait()
     x_down.wait()
 
@@ -143,22 +157,8 @@
         to_high[comp, tile] = turned[120:128]
 
     tiles(4, turn_wide)
-    wide_up = send(4, to_high, ghost_low, up_y)
-    wide_down = send(5, to_low, ghost_high, down_y)
-    y_up.wait()
-    y_down.wait()
-
-    def add_force(comp, tile):
-        middle = jnp.zeros((112, 128), jnp.float32)
-        turned = jnp.concatenate(
-            [from_low_y[comp, tile], middle, from_high_y[comp, tile]], axis=0
-        ).T
-        part = pl.ds(4 * tile, 4)
-        force[comp, part] = core[comp, part] + turned.reshape(4, 32, 128)
-
-    tiles(3, add_force)
-    force_up = send(6, force.at[:, 17:19], from_low_x, up_x)
-    force_down = send(7, force.at[:, 0:1], from_high_x, down_x)
+    wide_up = send(2, to_high, ghost_low, up_y)
+    wide_down = send(3, to_low, ghost_high, down_y)
     wide_up.wait()
     wide_down.wait()
 
@@ -200,38 +200,74 @@
 
     lax.fori_loop(1, 19, first_step, 0)
 
+    def second_step(x, carry):
+        def store(comp, value):
+            second[comp, x - 1] = value[:, 0:128]
+
+        relaxed(first, x, x + 1, store)
+        return carry
+
+    lax.fori_loop(1, 17, second_step, 0)
+
+
+def settle_kernel(
+    count_x, count_y, second, core, above, below,
+    final, field,
+    force, rim, from_low_y, from_high_y, from_low_x, from_high_x,
+    rim_up, rim_down, rim_low, rim_high, send_sems, recv_sems,
+):
+    up_x, down_x, up_y, down_y = neighbours(count_x, count_y)
+    greet((up_x, down_x, up_y, down_y))
+    send = sender(send_sems, recv_sems)
+    y_up = send(0, above, from_low_y, up_y)
+    y_down = send(1, below, from_high_y, down_y)
+    rim[:, 19:20] = jnp.zeros_like(rim[:, 19:20])
+    y_up.wait()
+    y_down.wait()
+
+    def add_force(comp, tile):
+        middle = jnp.zeros((112, 128), jnp.float32)
+        turned = jnp.concatenate(
+            [from_low_y[comp, tile], middle, from_high_y[comp, tile]], axis=0
+        ).T
+        part = pl.ds(4 * tile, 4)
+        force[comp, part] = core[comp, part] + turned.reshape(4, 32, 128)
+
+    tiles(3, add_force)
+    force_up = send(2, force.at[:, 17:19], from_low_x, up_x)
+    force_down = send(3, force.at[:, 0:1], from_high_x, down_x)
+
+    def finish(x, extra):
+        for comp in range(3):
+            total = second[comp, x - 1] + (force[comp, x] + extra(comp))
+            final[comp, x - 1] = total
+            rim[comp, x] = total.astype(jnp.bfloat16)
+
+    def middle_rows(x, carry):
+        finish(x, lambda comp: 0.0)
+        return carry
+
+    lax.fori_loop(3, 16, middle_rows, 0)
     force_up.wait()
     force_down.wait()
-    force[:, 1:3] = force[:, 1:3] + from_low_x[...]
-    force[:, 16:17] = force[:, 16:17] + from_high_x[...]
-
-    def second_step(x, carry):
-        def store(comp, value):
-            total = value[:, 0:128] + force[comp, x]
-            final[comp, x - 1] = total
-            rim[comp, x] = total.astype(jnp.bfloat16)
-
-        relaxed(first, x, x + 1, store)
-        return carry
-
-    lax.fori_loop(1, 17, second_step, 0)
-
-    rim_x_up = send(8, rim.at[:, 16:17], rim.at[:, 0:1], up_x)
-    rim_x_down = send(9, rim.at[:, 1:3], rim.at[:, 17:19], down_x)
+    finish(1, lambda comp: from_low_x[comp, 0])
+    finish(2, lambda comp: from_low_x[comp, 1])
+    finish(16, lambda comp: from_high_x[comp, 0])
+    rim_x_up = send(4, rim.at[:, 16:17], rim.at[:, 0:1], up_x)
+    rim_x_down = send(5, rim.at[:, 1:3], rim.at[:, 17:19], down_x)
     rim_x_up.wait()
     rim_x_down.wait()
 
     def turn_rim(comp, tile):
-        part = pl.ds(4 * tile, 4)
-        rows = rim[comp, part]
-        field[comp, part, :, 0:128] = rows
-        turned = rows.astype(jnp.float32).reshape(128, 128).T
+        turned = rim[comp, pl.ds(4 * tile, 4)].astype(jnp.float32).reshape(128, 128).T
         rim_down[comp, tile] = turned[0:8]
         rim_up[comp, tile] = turned[120:128]
 
     tiles(3, turn_rim)
-    rim_y_up = send(10, rim_up, rim_low, up_y)
-    rim_y_down = send(11, rim_down, rim_high, down_y)
+    rim_y_up = send(6, rim_up, rim_low, up_y)
+    rim_y_down = send(7, rim_down, rim_high, down_y)
+    for comp in range(3):
+        field[comp, :, :, 0:128] = rim[comp]
     rim_y_up.wait()
     rim_y_down.wait()
 
@@ -245,12 +281,39 @@
     tiles(3, fill_field)
 
 
-def settle(stacked, core, above, below):
+def ghosts(comps):
+    return pltpu.VMEM((comps, 5, 8, 128), jnp.float32)
+
+
+def flow(stacked):
     vmem = pl.BlockSpec(memory_space=pltpu.VMEM)
-
-    def ghosts(comps):
-        return pltpu.VMEM((comps, 5, 8, 128), jnp.float32)
-
+    return pl.pallas_call(
+        functools.partial(flow_kernel, lax.axis_size("gx"), lax.axis_size("gy")),
+        in_specs=[vmem],
+        out_specs=vmem,
+        out_shape=jax.ShapeDtypeStruct((3, 16, 32, 128), jnp.float32),
+        scratch_shapes=[
+            pltpu.VMEM((4, 20, 32, 256), jnp.float32),
+            pltpu.VMEM((3, 18, 32, 256), jnp.float32),
+            ghosts(4),
+            ghosts(4),
+            ghosts(4),
+            ghosts(4),
+            pltpu.SemaphoreType.DMA((4,)),
+            pltpu.SemaphoreType.DMA((4,)),
+        ],
+        compiler_params=pltpu.CompilerParams(
+            collective_id=1, has_side_effects=True, vmem_limit_bytes=32 * 2**20
+        ),
+        cost_estimate=pl.CostEstimate(
+            flops=10**7, bytes_accessed=4 * 10**7, transcendentals=0
+        ),
+        name="flow",
+    )(stacked)
+
+
+def settle(second, core, above, below):
+    vmem = pl.BlockSpec(memory_space=pltpu.VMEM)
     return pl.pallas_call(
         functools.partial(settle_kernel, lax.axis_size("gx"), lax.axis_size("gy")),
         in_specs=[vmem] * 4,
@@ -260,30 +323,24 @@
             jax.ShapeDtypeStruct((3, 20, 32, 256), jnp.bfloat16),
         ],
         scratch_shapes=[
-            pltpu.VMEM((4, 20, 32, 256), jnp.float32),
-            pltpu.VMEM((3, 18, 32, 256), jnp.float32),
             pltpu.VMEM((3, 20, 32, 128), jnp.float32),
             pltpu.VMEM((3, 20, 32, 128), jnp.bfloat16),
             ghosts(3),
             ghosts(3),
             pltpu.VMEM((3, 2, 32, 128), jnp.float32),
             pltpu.VMEM((3, 1, 32, 128), jnp.float32),
-            ghosts(4),
-            ghosts(4),
-            ghosts(4),
-            ghosts(4),
-            ghosts(3),
-            ghosts(3),
-            ghosts(3),
-            ghosts(3),
-            pltpu.SemaphoreType.DMA((12,)),
-            pltpu.SemaphoreType.DMA((12,)),
+            ghosts(3),
+            ghosts(3),
+            ghosts(3),
+            ghosts(3),
+            pltpu.SemaphoreType.DMA((8,)),
+            pltpu.SemaphoreType.DMA((8,)),
         ],
         compiler_params=pltpu.CompilerParams(
-            collective_id=0, has_side_effects=True, vmem_limit_bytes=40 * 2**20
+            collective_id=0, has_side_effects=True, vmem_limit_bytes=32 * 2**20
         ),
         name="settle",
-    )(stacked, core, above, below)
+    )(second, core, above, below)
 
 
 def body(velocity, viscosity, marker_cells, marker_offset, marker_force):
@@ -326,9 +383,9 @@
         spread_kernel,
         grid=(steps,),
         in_specs=[
-            pl.BlockSpec((3, GROUP, markers), lambda g: (0, g, 0)),
-            pl.BlockSpec((12, GROUP, markers), lambda g: (0, g, 0)),
-            pl.BlockSpec((3, GROUP, markers), lambda g: (0, g, 0)),
+            pl.BlockSpec(memory_space=pltpu.VMEM),
+            pl.BlockSpec(memory_space=pltpu.VMEM),
+            pl.BlockSpec(memory_space=pltpu.VMEM),
         ],
         out_specs=[
             pl.BlockSpec((3, 640, 128), lambda g: (0, 0, 0)),
@@ -350,29 +407,34 @@
             pltpu.VMEM((rows, lanes), jnp.bfloat16),
             pltpu.VMEM((3, 640, 256), jnp.float32),
         ],
+        compiler_params=pltpu.CompilerParams(vmem_limit_bytes=24 * 2**20),
         name="spread",
-    )(cells, weights, forces)
+    )(
+        cells.reshape(3, steps, GROUP, markers),
+        weights.reshape(12, steps, GROUP, markers),
+        forces.reshape(3, steps, GROUP, markers),
+    )
 
     stacked = jnp.concatenate([velocity, viscosity[None]], axis=0)
     stacked = jnp.swapaxes(stacked, 1, 2)
-    final, field = settle(stacked, core.reshape(3, 20, depth, width_y), above, below)
+    second = flow(stacked)
+    final, field = settle(second, core.reshape(3, 20, depth, width_y), above, below)
     field = field.reshape(3, 640, 256)
 
     sampled = pl.pallas_call(
         sample_kernel,
         grid=(steps,),
         in_specs=[
-            pl.BlockSpec((3, 640, 256), lambda g: (0, 0, 0)),
+            pl.BlockSpec(memory_space=pltpu.VMEM),
             pl.BlockSpec((1, YR, lanes), lambda g: (g, 0, 0)),
             pl.BlockSpec((1, 24, lanes), lambda g: (g, 0, 0)),
             pl.BlockSpec((1, depth, lanes), lambda g: (g, 0, 0)),
         ],
-        out_specs=pl.BlockSpec((1, 3, lanes), lambda g: (g, 0, 0)),
-        out_shape=jax.ShapeDtypeStruct((steps, 3, lanes), jnp.float32),
+        out_specs=pl.BlockSpec((GROUP // CAP, CAP * 3, markers), lambda g: (g, 0, 0)),
+        out_shape=jax.ShapeDtypeStruct((column_size, CAP * 3, markers), jnp.float32),
+        compiler_params=pltpu.CompilerParams(vmem_limit_bytes=24 * 2**20),
         name="sample",
     )(field, y_matrix, x_matrix, z_matrix)
-    sampled = jnp.swapaxes(sampled.reshape(steps, 3, GROUP, markers), 1, 2)
-    sampled = sampled.reshape(column_size, CAP * 3, markers)
     returned = lax.all_to_all(sampled, "gy", 0, 0, tiled=True).reshape(slots, -1)
     marker_velocity = jnp.dot(place.T, returned, precision=lax.Precision.HIGHEST)
     return (jnp.swapaxes(final, 1, 2), marker_velocity.reshape(blocks, 3, markers))

time: 122 us -> 119 us (0.975)
  Pallas kernels: 59.9 us -> 78 us
  waiting for transfers between devices: 23.9 us -> 10 us
  local copies, waits for them, and re-layouts: 10.7 us -> 4.52 us
    pallas_call x2 -> x3, Pallas kernels: 28.5 us -> 51.9 us  [the longest x1 27.2 us: flow(): pl.pallas_call(functools.partial(flow_kernel, lax.axis_size('gx'), lax.ax...]
    all_to_all x1, waiting for transfers between devices: 14.6 us -> 0.01 us  [body(): received = lax.all_to_all(sent, 'gy', 0, 0, tiled=True)]
    pallas_call x1, Pallas kernels: 31.4 us -> 26.1 us  [settle(): pl.pallas_call(functools.partial(settle_kernel, lax.axis_size('gx'), lax....]
    unnamed x15 -> x5, local copies, waits for them, and re-layouts: 7.17 us -> 2.64 us
    reshape x2 -> x0, local copies, waits for them, and re-layouts: 1.65 us -> none  [the longest x1 0.96 us: body(): sampled = jnp.swapaxes(sampled.reshape(steps, 3, GROUP, markers), 1, 2)]
  transfers between devices with their start and end apart: 2 -> 2, of which waited for: 2 -> 1; matrix products, arithmetic and copies ran while one was open for 2% -> 2% of each run, Pallas kernels for 0% -> 23%
where the time goes in v3:
time: 119 us; the launch traced here: 118 us
  Pallas kernels  78 us (66%)
  starting transfers between devices  21.3 us (18%)
  waiting for transfers between devices  10 us (8%)
  local copies, waits for them, and re-layouts  4.52 us (4%)
  matrix products  2.06 us (2%)
  other arithmetic  1.63 us (1%)
    pallas_call x1, Pallas kernels, flow(): pl.pallas_call(functools.partial(flow_kernel, lax.axis_size('gx'), lax.ax...  27.2 us
    pallas_call x1, Pallas kernels, settle(): pl.pallas_call(functools.partial(settle_kernel, lax.axis_size('gx'), lax....  26.1 us
    pallas_call x1, Pallas kernels, body(): pl.pallas_call(spread_kernel, grid=(steps,), in_specs=[pl.BlockSpec(memor...  15 us
    all_to_all x1, starting transfers between devices, body(): received = lax.all_to_all(sent, 'gy', 0, 0, tiled=True)  12.8 us
    all_to_all x1, waiting for transfers between devices, body(): lax.all_to_all(sampled, 'gy', 0, 0, tiled=True).reshape(slots, -1)  10 us
    pallas_call x1, Pallas kernels, body(): pl.pallas_call(sample_kernel, grid=(steps,), in_specs=[pl.BlockSpec(memor...  9.78 us
    all_to_all x1, starting transfers between devices, body(): lax.all_to_all(sampled, 'gy', 0, 0, tiled=True).reshape(slots, -1)  8.55 us
    unnamed x5, local copies, waits for them, and re-layouts  2.64 us
  transfers between devices with their start and end apart: 2, of which 1 were waited for; matrix products, arithmetic and copies ran while one was open for 2% of the time, Pallas kernels for 23%

profile of v3, /device:TPU:1, one launch (start us, length us, event | category | flops | bytes accessed | tf_op | source)
XLA Modules:
  0.0 118.4 jit_solution(11910609014079160166)
XLA Ops:
  0.6 0.0 copy-start
  0.6 0.9 slice_reduce_fusion
  1.6 0.2 select_reduce_fusion
  1.8 0.8 slice_subtract_fusion.1
  2.6 1.2 %fusion = f32[64,1152]{1,0:T(8,128)S(1)} fusion(s32[32]{0:T(128)S(1)} %multiply_add_fusion.12, f32[32,3,128]{2,0,1:T(8,128)} %param.9, f32[32,3,128]{2,0,1:T(8,128)} %param.8, f32[32,3,128]{2,0,1:T(8,128)S(1)} %add_convert_fusion), kind=kOutput, calls=%fused_computation.3 | convolution fusion | flops 28387328 | bytes 442496 | tf_op jit(solution)/shard_map/dot_general | solution.py:370
  3.8 0.8 reshape.130
  4.7 12.8 %all-to-all-start = ((f32[32,18,128]{2,1,0:T(8,128)}), f32[32,18,128]{2,1,0:T(8,128)S(1)}, u32[]{:S(2)}, u32[]{:S(2)}) async-start(f32[32,18,128]{2,1,0:T(8,128)} %reshape.130), calls=%async_computation | async-start | bytes 786432 | tf_op jit(solution)/shard_map/all_to_all | solution.py:372
  17.4 1.0 copy.43
  18.5 0.0 copy-done
  18.5 0.3 copy.25
  18.7 0.1 maximum_bitcast_fusion.stacked
  18.8 27.2 %flow.1.second = f32[3,16,32,128]{3,2,1,0:T(8,128)S(1)} custom-call(f32[4,16,32,128]{3,2,1,0:T(8,128)S(1)} %maximum_bitcast_fusion.stacked), custom_call_target="tpu_custom_call" | custom-call | flops 10000000 | bytes 40000000 | tf_op jit(solution)/shard_map/flow/pallas_call | solution.py:290
  46.0 0.0 all-to-all-done
  46.0 0.1 copy.42
  46.7 15.0 %spread.1 = (f32[3,640,128]{2,1,0:T(8,128)S(1)}, f32[3,5,8,128]{3,2,1,0:T(8,128)S(1)}, f32[3,5,8,128]{3,2,1,0:T(8,128)S(1)}, bf16[8,144,1024]{2,1,0:T(8,128)(2,1...) custom-call(s32[3,8,8,128]{3,2,1,0:T(8,128)S(1)} %get-tuple-element.29.cells, ...), custom_call_target="tpu_custom_call" | custom-call | tf_op jit(solution)/shard_map/spread/pallas_call | solution.py:382
  61.7 26.1 %settle.1 = (f32[3,16,32,128]{3,2,1,0:T(8,128)S(1)}, bf16[3,20,32,256]{3,2,1,0:T(8,128)(2,1)S(1)}) custom-call(f32[3,16,32,128]{3,2,1,0:T(8,128)S(1)} %flow.1.second, f32[3,20,32,128]{3,2,1,0:T(8,128)S(1)} %bitcast.82, f32[3,5,8,128]{3,2,1,0:T(8,128)S(1)} %get-tuple-element.11.above, f32[3,5,8,128]{3,2,1,0:T(8,128)S(1)} %get-tuple-element.12.below), custom_call_target="tpu_custom_call" | custom-call | tf_op jit(solution)/shard_map/settle/pallas_call | solution.py:317
  87.8 9.8 %sample.1 = f32[32,6,128]{2,1,0:T(8,128)} custom-call(bf16[3,640,256]{2,1,0:T(8,128)(2,1)S(1)} %bitcast.81, bf16[8,144,1024]{2,1,0:T(8,128)(2,1)S(1)} %get-tuple-element.15.y_ref, f32[8,24,1024]{2,1,0:T(8,128)S(1)} %get-tuple-element.16.x_ref, f32[8,32,1024]{2,1,0:T(8,128)S(1)} %get-tuple-element.17.z_ref), custom_call_target="tpu_custom_call" | custom-call | tf_op jit(solution)/shard_map/sample/pallas_call | solution.py:424
  97.6 8.5 %all-to-all-start.1 = ((f32[32,6,128]{2,1,0:T(8,128)}), f32[32,6,128]{2,1,0:T(8,128)S(1)}, u32[]{:S(2)}, u32[]{:S(2)}) async-start(f32[32,6,128]{2,1,0:T(8,128)} %sample.1), calls=%async_computation.1 | async-start | bytes 262144 | tf_op jit(solution)/shard_map/all_to_all | solution.py:438
  106.2 1.3 %copy.29 = f32[3,32,16,128]{3,2,1,0:T(8,128)} copy(f32[3,32,16,128]{3,1,2,0:T(8,128)S(1)} %bitcast.83) | data formatting | bytes 1572864
  107.5 10.0 %all-to-all-done.1 = f32[32,6,128]{2,1,0:T(8,128)S(1)} async-done(((f32[32,6,128]{2,1,0:T(8,128)}), f32[32,6,128]{2,1,0:T(8,128)S(1)}, u32[]{:S(2)}, u32[]{:S(2)}) %all-to-all-start.1) | async-done | bytes 98336 | tf_op jit(solution)/shard_map/all_to_all | solution.py:438
  117.6 0.8 fusion.3
  (18 shorter events, 0.6 us)
Async XLA Ops:
  0.6 17.8 %copy-start = (f32[3,32,16,128]{3,2,1,0:T(8,128)S(1)}, f32[3,32,16,128]{3,2,1,0:T(8,128)}, u32[]{:S(2)}) copy-start(f32[3,32,16,128]{3,2,1,0:T(8,128)} %param.5) | copy-start | bytes 2359300
  4.7 41.3 %all-to-all-start = ((f32[32,18,128]{2,1,0:T(8,128)}), f32[32,18,128]{2,1,0:T(8,128)S(1)}, u32[]{:S(2)}, u32[]{:S(2)}) async-start(f32[32,18,128]{2,1,0:T(8,128)} %reshape.130), calls=%async_computation | async-start | bytes 786432 | tf_op jit(solution)/shard_map/all_to_all | solution.py:372
  97.6 19.9 %all-to-all-start.1 = ((f32[32,6,128]{2,1,0:T(8,128)}), f32[32,6,128]{2,1,0:T(8,128)S(1)}, u32[]{:S(2)}, u32[]{:S(2)}) async-start(f32[32,6,128]{2,1,0:T(8,128)} %sample.1), calls=%async_computation.1 | async-start | bytes 262144 | tf_op jit(solution)/shard_map/all_to_all | solution.py:438

commit v4 on v3

--- a/solution.py
+++ b/solution.py
@@ -131,11 +131,70 @@
 
 
 def tiles(comps, body):
-    def step(index, carry):
-        body(index // 5, lax.rem(index, 5))
+    def step(tile, carry):
+        for comp in range(comps):
+            body(comp, tile)
         return carry
 
-    lax.fori_loop(0, comps * 5, step, 0)
+    lax.fori_loop(0, 5, step, 0)
+
+
+def all_peers(count, body):
+    me_x, me_y = lax.axis_index("gx"), lax.axis_index("gy")
+
+    def step(distance, carry):
+        peer = lax.rem(me_y + distance, count)
+        body(distance, peer, (me_x, peer))
+        return carry
+
+    lax.fori_loop(1, count, step, 0)
+
+
+def exchange_copy(source, target, send_sems, recv_sems, distance, peer, device):
+    return pltpu.make_async_remote_copy(
+        src_ref=source.at[peer],
+        dst_ref=target.at[lax.axis_index("gy")],
+        send_sem=send_sems.at[distance],
+        recv_sem=recv_sems.at[distance],
+        device_id=device,
+        device_id_type=MESH,
+    )
+
+
+def return_kernel(count, source, target, send_sems, recv_sems):
+    me = lax.axis_index("gy")
+    barrier = pltpu.get_barrier_semaphore()
+
+    def greet_peer(distance, peer, device):
+        pl.semaphore_signal(barrier, inc=1, device_id=device, device_id_type=MESH)
+
+    def start(*where):
+        exchange_copy(source, target, send_sems, recv_sems, *where).start()
+
+    def finish(*where):
+        exchange_copy(source, target, send_sems, recv_sems, *where).wait()
+
+    all_peers(count, greet_peer)
+    pl.semaphore_wait(barrier, count - 1)
+    all_peers(count, start)
+    target[me] = source[me]
+    all_peers(count, finish)
+
+
+def send_back(rows):
+    count = lax.axis_size("gy")
+    vmem = pl.BlockSpec(memory_space=pltpu.VMEM)
+    return pl.pallas_call(
+        functools.partial(return_kernel, count),
+        in_specs=[vmem],
+        out_specs=vmem,
+        out_shape=jax.ShapeDtypeStruct(rows.shape, rows.dtype),
+        scratch_shapes=[pltpu.SemaphoreType.DMA((count,)), pltpu.SemaphoreType.DMA((count,))],
+        compiler_params=pltpu.CompilerParams(
+            collective_id=2, has_side_effects=True, vmem_limit_bytes=32 * 2**20
+        ),
+        name="send_back",
+    )(rows)
 
 
 def flow_kernel(
@@ -435,7 +494,7 @@
         compiler_params=pltpu.CompilerParams(vmem_limit_bytes=24 * 2**20),
         name="sample",
     )(field, y_matrix, x_matrix, z_matrix)
-    returned = lax.all_to_all(sampled, "gy", 0, 0, tiled=True).reshape(slots, -1)
+    returned = send_back(sampled).reshape(slots, -1)
     marker_velocity = jnp.dot(place.T, returned, precision=lax.Precision.HIGHEST)
     return (jnp.swapaxes(final, 1, 2), marker_velocity.reshape(blocks, 3, markers))
 

time: 119 us -> 107 us (0.90)
  waiting for transfers between devices: 10 us -> 0.01 us
  starting transfers between devices: 21.3 us -> 12.8 us
  Pallas kernels: 78 us -> 84.7 us
    pallas_call x0 -> x1, Pallas kernels: none -> 13 us  [send_back(): pl.pallas_call(functools.partial(return_kernel, count), in_specs=[vmem],...]
    all_to_all x1 -> x0, waiting for transfers between devices: 10 us -> none  [body(): lax.all_to_all(sampled, 'gy', 0, 0, tiled=True).reshape(slots, -1)]
    all_to_all x1 -> x0, starting transfers between devices: 8.55 us -> none  [body(): lax.all_to_all(sampled, 'gy', 0, 0, tiled=True).reshape(slots, -1)]
    pallas_call x1, Pallas kernels: 26.1 us -> 23.1 us  [settle(): pl.pallas_call(functools.partial(settle_kernel, lax.axis_size('gx'), lax....]
    pallas_call x1, Pallas kernels: 27.2 us -> 24.5 us  [flow(): pl.pallas_call(functools.partial(flow_kernel, lax.axis_size('gx'), lax.ax...]
  transfers between devices with their start and end apart: 2 -> 1, of which waited for: 1 -> 0; matrix products, arithmetic and copies ran while one was open for 2% -> 1% of each run, Pallas kernels for 23% -> 23%
where the time goes in v4:
time: 107 us
  Pallas kernels  84.7 us (79%)
  starting transfers between devices  12.8 us (12%)
  local copies, waits for them, and re-layouts  4.53 us (4%)
  matrix products  2.06 us (2%)
  other arithmetic  1.63 us (2%)
    pallas_call x1, Pallas kernels, flow(): pl.pallas_call(functools.partial(flow_kernel, lax.axis_size('gx'), lax.ax...  24.5 us
    pallas_call x1, Pallas kernels, settle(): pl.pallas_call(functools.partial(settle_kernel, lax.axis_size('gx'), lax....  23.1 us
    pallas_call x1, Pallas kernels, body(): pl.pallas_call(spread_kernel, grid=(steps,), in_specs=[pl.BlockSpec(memor...  15 us
    pallas_call x1, Pallas kernels, send_back(): pl.pallas_call(functools.partial(return_kernel, count), in_specs=[vmem],...  13 us
    all_to_all x1, starting transfers between devices, body(): received = lax.all_to_all(sent, 'gy', 0, 0, tiled=True)  12.8 us
    pallas_call x1, Pallas kernels, body(): pl.pallas_call(sample_kernel, grid=(steps,), in_specs=[pl.BlockSpec(memor...  9.14 us
    unnamed x5, local copies, waits for them, and re-layouts  2.64 us
  transfers between devices with their start and end apart: 1, of which 0 were waited for; matrix products, arithmetic and copies ran while one was open for 1% of the time, Pallas kernels for 23%

profile of v4, /device:TPU:1, one launch (start us, length us, event | category | flops | bytes accessed | tf_op | source)
XLA Modules:
  0.0 106.6 jit_solution(17272427358474704083)
XLA Ops:
  0.6 0.0 copy-start
  0.6 0.9 slice_reduce_fusion
  1.6 0.2 select_reduce_fusion
  1.8 0.8 slice_subtract_fusion.1
  2.6 1.2 %fusion = f32[64,1152]{1,0:T(8,128)S(1)} fusion(s32[32]{0:T(128)S(1)} %multiply_add_fusion.12, f32[32,3,128]{2,0,1:T(8,128)} %param.9, f32[32,3,128]{2,0,1:T(8,128)} %param.8, f32[32,3,128]{2,0,1:T(8,128)S(1)} %add_convert_fusion), kind=kOutput, calls=%fused_computation.3 | convolution fusion | flops 28387328 | bytes 442496 | tf_op jit(solution)/shard_map/dot_general | solution.py:429
  3.8 0.8 reshape.130
  4.7 12.8 %all-to-all-start = ((f32[32,18,128]{2,1,0:T(8,128)}), f32[32,18,128]{2,1,0:T(8,128)S(1)}, u32[]{:S(2)}, u32[]{:S(2)}) async-start(f32[32,18,128]{2,1,0:T(8,128)} %reshape.130), calls=%async_computation | async-start | bytes 786432 | tf_op jit(solution)/shard_map/all_to_all | solution.py:431
  17.4 1.0 copy.43
  18.5 0.0 copy-done
  18.5 0.3 copy.25
  18.7 0.1 maximum_bitcast_fusion.stacked
  18.8 24.5 %flow.1.second = f32[3,16,32,128]{3,2,1,0:T(8,128)S(1)} custom-call(f32[4,16,32,128]{3,2,1,0:T(8,128)S(1)} %maximum_bitcast_fusion.stacked), custom_call_target="tpu_custom_call" | custom-call | flops 10000000 | bytes 40000000 | tf_op jit(solution)/shard_map/flow/pallas_call | solution.py:349
  43.3 0.0 all-to-all-done
  43.4 0.1 copy.42
  44.1 15.0 %spread.1 = (f32[3,640,128]{2,1,0:T(8,128)S(1)}, f32[3,5,8,128]{3,2,1,0:T(8,128)S(1)}, f32[3,5,8,128]{3,2,1,0:T(8,128)S(1)}, bf16[8,144,1024]{2,1,0:T(8,128)(2,1...) custom-call(s32[3,8,8,128]{3,2,1,0:T(8,128)S(1)} %get-tuple-element.29.cells, ...), custom_call_target="tpu_custom_call" | custom-call | tf_op jit(solution)/shard_map/spread/pallas_call | solution.py:441
  59.1 23.1 %settle.1 = (f32[3,16,32,128]{3,2,1,0:T(8,128)S(1)}, bf16[3,20,32,256]{3,2,1,0:T(8,128)(2,1)S(1)}) custom-call(f32[3,16,32,128]{3,2,1,0:T(8,128)S(1)} %flow.1.second, f32[3,20,32,128]{3,2,1,0:T(8,128)S(1)} %bitcast.82, f32[3,5,8,128]{3,2,1,0:T(8,128)S(1)} %get-tuple-element.11.above, f32[3,5,8,128]{3,2,1,0:T(8,128)S(1)} %get-tuple-element.12.below), custom_call_target="tpu_custom_call" | custom-call | tf_op jit(solution)/shard_map/settle/pallas_call | solution.py:376
  82.2 1.3 %copy.29 = f32[3,32,16,128]{3,2,1,0:T(8,128)} copy(f32[3,32,16,128]{3,1,2,0:T(8,128)S(1)} %bitcast.83) | data formatting | bytes 1572864
  83.5 9.1 %sample.1.source = f32[32,6,128]{2,1,0:T(8,128)S(1)} custom-call(bf16[3,640,256]{2,1,0:T(8,128)(2,1)S(1)} %bitcast.81, bf16[8,144,1024]{2,1,0:T(8,128)(2,1)S(1)} %get-tuple-element.15.y_ref, f32[8,24,1024]{2,1,0:T(8,128)S(1)} %get-tuple-element.16.x_ref, f32[8,32,1024]{2,1,0:T(8,128)S(1)} %get-tuple-element.17.z_ref), custom_call_target="tpu_custom_call" | custom-call | tf_op jit(solution)/shard_map/sample/pallas_call | solution.py:483
  92.7 13.0 %send_back.1 = f32[32,6,128]{2,1,0:T(8,128)S(1)} custom-call(f32[32,6,128]{2,1,0:T(8,128)S(1)} %sample.1.source), custom_call_target="tpu_custom_call" | custom-call | tf_op jit(solution)/shard_map/send_back/pallas_call | solution.py:187
  105.7 0.8 fusion.3
  (18 shorter events, 0.6 us)
Async XLA Ops:
  0.6 17.8 %copy-start = (f32[3,32,16,128]{3,2,1,0:T(8,128)S(1)}, f32[3,32,16,128]{3,2,1,0:T(8,128)}, u32[]{:S(2)}) copy-start(f32[3,32,16,128]{3,2,1,0:T(8,128)} %param.5) | copy-start | bytes 2359300
  4.7 38.7 %all-to-all-start = ((f32[32,18,128]{2,1,0:T(8,128)}), f32[32,18,128]{2,1,0:T(8,128)S(1)}, u32[]{:S(2)}, u32[]{:S(2)}) async-start(f32[32,18,128]{2,1,0:T(8,128)} %reshape.130), calls=%async_computation | async-start | bytes 786432 | tf_op jit(solution)/shard_map/all_to_all | solution.py:431

commit v5 on v4

--- a/solution.py
+++ b/solution.py
@@ -198,14 +198,32 @@
 
 
 def flow_kernel(
-    count_x, count_y, stacked, second, wide, first, to_high, to_low, ghost_low, ghost_high,
-    send_sems, recv_sems,
+    count_x, count_y, stacked, sent, second, received,
+    wide, first, to_high, to_low, ghost_low, ghost_high,
+    send_sems, recv_sems, block_send_sems, block_recv_sems,
 ):
+    me = lax.axis_index("gy")
     up_x, down_x, up_y, down_y = neighbours(count_x, count_y)
-    greet((up_x, down_x, up_y, down_y))
+    barrier = pltpu.get_barrier_semaphore()
+
+    def greet_peer(distance, peer, device):
+        pl.semaphore_signal(barrier, inc=1, device_id=device, device_id_type=MESH)
+
+    def start_block(*where):
+        exchange_copy(sent, received, block_send_sems, block_recv_sems, *where).start()
+
+    def finish_block(*where):
+        exchange_copy(sent, received, block_send_sems, block_recv_sems, *where).wait()
+
+    for device in (up_x, down_x):
+        pl.semaphore_signal(barrier, inc=1, device_id=device, device_id_type=MESH)
+    all_peers(count_y, greet_peer)
+    pl.semaphore_wait(barrier, count_y + 1)
     send = sender(send_sems, recv_sems)
     x_up = send(0, stacked.at[:, 14:16], wide.at[:, 0:2, :, 0:128], up_x)
     x_down = send(1, stacked.at[:, 0:2], wide.at[:, 18:20, :, 0:128], down_x)
+    all_peers(count_y, start_block)
+    received[me] = sent[me]
     wide[:, 2:18, :, 0:128] = stacked[...]
     x_up.wait()
     x_down.wait()
@@ -267,6 +285,7 @@
         return carry
 
     lax.fori_loop(1, 17, second_step, 0)
+    all_peers(count_y, finish_block)
 
 
 def settle_kernel(
@@ -344,13 +363,17 @@
     return pltpu.VMEM((comps, 5, 8, 128), jnp.float32)
 
 
-def flow(stacked):
+def flow(stacked, sent):
+    count_y = lax.axis_size("gy")
     vmem = pl.BlockSpec(memory_space=pltpu.VMEM)
     return pl.pallas_call(
-        functools.partial(flow_kernel, lax.axis_size("gx"), lax.axis_size("gy")),
-        in_specs=[vmem],
-        out_specs=vmem,
-        out_shape=jax.ShapeDtypeStruct((3, 16, 32, 128), jnp.float32),
+        functools.partial(flow_kernel, lax.axis_size("gx"), count_y),
+        in_specs=[vmem] * 2,
+        out_specs=[vmem] * 2,
+        out_shape=[
+            jax.ShapeDtypeStruct((3, 16, 32, 128), jnp.float32),
+            jax.ShapeDtypeStruct(sent.shape, sent.dtype),
+        ],
         scratch_shapes=[
             pltpu.VMEM((4, 20, 32, 256), jnp.float32),
             pltpu.VMEM((3, 18, 32, 256), jnp.float32),
@@ -360,6 +383,8 @@
             ghosts(4),
             pltpu.SemaphoreType.DMA((4,)),
             pltpu.SemaphoreType.DMA((4,)),
+            pltpu.SemaphoreType.DMA((count_y,)),
+            pltpu.SemaphoreType.DMA((count_y,)),
         ],
         compiler_params=pltpu.CompilerParams(
             collective_id=1, has_side_effects=True, vmem_limit_bytes=32 * 2**20
@@ -368,7 +393,7 @@
             flops=10**7, bytes_accessed=4 * 10**7, transcendentals=0
         ),
         name="flow",
-    )(stacked)
+    )(stacked, sent)
 
 
 def settle(second, core, above, below):
@@ -428,7 +453,9 @@
     packed = jnp.concatenate([local.astype(jnp.float32), marker_offset, marker_force], axis=1)
     sent = jnp.dot(place, packed.reshape(blocks, -1), precision=lax.Precision.HIGHEST)
     sent = sent.reshape(column_size, CAP * 9, markers)
-    received = lax.all_to_all(sent, "gy", 0, 0, tiled=True)
+    stacked = jnp.concatenate([velocity, viscosity[None]], axis=0)
+    stacked = jnp.swapaxes(stacked, 1, 2)
+    second, received = flow(stacked, sent)
     received = jnp.moveaxis(received.reshape(slots, 9, markers), 1, 0)
     cells = received[0:3].astype(jnp.int32)
     weights = jnp.stack(
@@ -474,9 +501,6 @@
         forces.reshape(3, steps, GROUP, markers),
     )
 
-    stacked = jnp.concatenate([velocity, viscosity[None]], axis=0)
-    stacked = jnp.swapaxes(stacked, 1, 2)
-    second = flow(stacked)
     final, field = settle(second, core.reshape(3, 20, depth, width_y), above, below)
     field = field.reshape(3, 640, 256)
 

time: 107 us -> 101 us (0.944)
  starting transfers between devices: 12.8 us -> 0 us
  Pallas kernels: 84.7 us -> 91.9 us
    all_to_all x1 -> x0, starting transfers between devices: 12.8 us -> none  [body(): received = lax.all_to_all(sent, 'gy', 0, 0, tiled=True)]
    pallas_call x1, Pallas kernels: 24.5 us -> 30.8 us  [flow(): pl.pallas_call(functools.partial(flow_kernel, lax.axis_size('gx'), count_...]
    pallas_call x1, Pallas kernels: 13 us -> 16.7 us  [send_back(): pl.pallas_call(functools.partial(return_kernel, count), in_specs=[vmem],...]
    pallas_call x1, Pallas kernels: 23.1 us -> 20.3 us  [settle(): pl.pallas_call(functools.partial(settle_kernel, lax.axis_size('gx'), lax....]
  transfers between devices with their start and end apart: 1 -> 0, of which waited for: 0 -> 0; matrix products, arithmetic and copies ran while one was open for 1% -> 0% of each run, Pallas kernels for 23% -> 0%
where the time goes in v5:
time: 101 us; the launch traced here: 100 us
  Pallas kernels  91.9 us (91%)
  local copies, waits for them, and re-layouts  3.78 us (4%)
  matrix products  2.06 us (2%)
  other arithmetic  1.63 us (2%)
    pallas_call x1, Pallas kernels, flow(): pl.pallas_call(functools.partial(flow_kernel, lax.axis_size('gx'), count_...  30.8 us
    pallas_call x1, Pallas kernels, settle(): pl.pallas_call(functools.partial(settle_kernel, lax.axis_size('gx'), lax....  20.3 us
    pallas_call x1, Pallas kernels, send_back(): pl.pallas_call(functools.partial(return_kernel, count), in_specs=[vmem],...  16.7 us
    pallas_call x1, Pallas kernels, body(): pl.pallas_call(spread_kernel, grid=(steps,), in_specs=[pl.BlockSpec(memor...  15 us
    pallas_call x1, Pallas kernels, body(): pl.pallas_call(sample_kernel, grid=(steps,), in_specs=[pl.BlockSpec(memor...  9.13 us
    unnamed x5, local copies, waits for them, and re-layouts  2.64 us

profile of v5, /device:TPU:1, one launch (start us, length us, event | category | flops | bytes accessed | tf_op | source)
XLA Modules:
  0.0 100.2 jit_solution(7921036680880007204)
XLA Ops:
  0.6 0.0 copy-start
  0.6 0.9 slice_reduce_fusion
  1.6 0.2 select_reduce_fusion
  1.8 0.8 slice_subtract_fusion.1
  2.6 1.2 %fusion = f32[64,1152]{1,0:T(8,128)S(1)} fusion(s32[32]{0:T(128)S(1)} %multiply_add_fusion.12, f32[32,3,128]{2,0,1:T(8,128)} %param.9, f32[32,3,128]{2,0,1:T(8,128)} %param.8, f32[32,3,128]{2,0,1:T(8,128)S(1)} %add_convert_fusion), kind=kOutput, calls=%fused_computation.3 | convolution fusion | flops 28387328 | bytes 442496 | tf_op jit(solution)/shard_map/dot_general | solution.py:454
  3.8 0.1 reshape.130.sent
  3.9 1.0 %copy.44 = f32[32,16,128]{2,0,1:T(8,128)S(1)} copy(f32[32,16,128]{2,1,0:T(8,128)} %param.6) | data formatting | bytes 524288 | tf_op args[1]
  5.0 0.0 copy-done
  5.0 0.3 copy.26
  5.2 0.1 maximum_bitcast_fusion.stacked
  5.3 30.8 %flow.1 = (f32[3,16,32,128]{3,2,1,0:T(8,128)S(1)}, f32[32,18,128]{2,1,0:T(8,128)S(1)}) custom-call(f32[4,16,32,128]{3,2,1,0:T(8,128)S(1)} %maximum_bitcast_fusion.stacked, f32[32,18,128]{2,1,0:T(8,128)S(1)} %reshape.130.sent), custom_call_target="tpu_custom_call" | custom-call | flops 10000000 | bytes 40000000 | tf_op jit(solution)/shard_map/flow/pallas_call | solution.py:369
  36.1 0.1 copy.43
  36.8 15.0 %spread.1 = (f32[3,640,128]{2,1,0:T(8,128)S(1)}, f32[3,5,8,128]{3,2,1,0:T(8,128)S(1)}, f32[3,5,8,128]{3,2,1,0:T(8,128)S(1)}, bf16[8,144,1024]{2,1,0:T(8,128)(2,1...) custom-call(s32[3,8,8,128]{3,2,1,0:T(8,128)S(1)} %get-tuple-element.33.cells, ...), custom_call_target="tpu_custom_call" | custom-call | tf_op jit(solution)/shard_map/spread/pallas_call | solution.py:468
  51.8 20.3 %settle.1 = (f32[3,16,32,128]{3,2,1,0:T(8,128)S(1)}, bf16[3,20,32,256]{3,2,1,0:T(8,128)(2,1)S(1)}) custom-call(f32[3,16,32,128]{3,2,1,0:T(8,128)S(1)} %get-tuple-element.12.second, f32[3,20,32,128]{3,2,1,0:T(8,128)S(1)} %bitcast.82, f32[3,5,8,128]{3,2,1,0:T(8,128)S(1)} %get-tuple-element.15.above, f32[3,5,8,128]{3,2,1,0:T(8,128)S(1)} %get-tuple-element.16.below), custom_call_target="tpu_custom_call" | custom-call | tf_op jit(solution)/shard_map/settle/pallas_call | solution.py:401
  72.1 1.3 %copy.30 = f32[3,32,16,128]{3,2,1,0:T(8,128)} copy(f32[3,32,16,128]{3,1,2,0:T(8,128)S(1)} %bitcast.83) | data formatting | bytes 1572864
  73.5 9.1 %sample.1.source = f32[32,6,128]{2,1,0:T(8,128)S(1)} custom-call(bf16[3,640,256]{2,1,0:T(8,128)(2,1)S(1)} %bitcast.81, bf16[8,144,1024]{2,1,0:T(8,128)(2,1)S(1)} %get-tuple-element.19.y_ref, f32[8,24,1024]{2,1,0:T(8,128)S(1)} %get-tuple-element.20.x_ref, f32[8,32,1024]{2,1,0:T(8,128)S(1)} %get-tuple-element.21.z_ref), custom_call_target="tpu_custom_call" | custom-call | tf_op jit(solution)/shard_map/sample/pallas_call | solution.py:507
  82.6 16.7 %send_back.1 = f32[32,6,128]{2,1,0:T(8,128)S(1)} custom-call(f32[32,6,128]{2,1,0:T(8,128)S(1)} %sample.1.source), custom_call_target="tpu_custom_call" | custom-call | tf_op jit(solution)/shard_map/send_back/pallas_call | solution.py:187
  99.4 0.8 fusion.3
  (18 shorter events, 0.6 us)
Async XLA Ops:
  0.6 4.3 %copy-start = (f32[3,32,16,128]{3,2,1,0:T(8,128)S(1)}, f32[3,32,16,128]{3,2,1,0:T(8,128)}, u32[]{:S(2)}) copy-start(f32[3,32,16,128]{3,2,1,0:T(8,128)} %param.5) | copy-start | bytes 2359300

commit v6 on v5

--- a/solution.py
+++ b/solution.py
@@ -222,8 +222,6 @@
     send = sender(send_sems, recv_sems)
     x_up = send(0, stacked.at[:, 14:16], wide.at[:, 0:2, :, 0:128], up_x)
     x_down = send(1, stacked.at[:, 0:2], wide.at[:, 18:20, :, 0:128], down_x)
-    all_peers(count_y, start_block)
-    received[me] = sent[me]
     wide[:, 2:18, :, 0:128] = stacked[...]
     x_up.wait()
     x_down.wait()
@@ -236,6 +234,8 @@
     tiles(4, turn_wide)
     wide_up = send(2, to_high, ghost_low, up_y)
     wide_down = send(3, to_low, ghost_high, down_y)
+    all_peers(count_y, start_block)
+    received[me] = sent[me]
     wide_up.wait()
     wide_down.wait()
 

time: 101 us -> 103 us (1.020)
  Pallas kernels: 91.9 us -> 94 us
    pallas_call x1, Pallas kernels: 20.3 us -> 22.9 us  [settle(): pl.pallas_call(functools.partial(settle_kernel, lax.axis_size('gx'), lax....]
    pallas_call x1, Pallas kernels: 30.8 us -> 29.6 us  [flow(): pl.pallas_call(functools.partial(flow_kernel, lax.axis_size('gx'), count_...]
where the time goes in v6:
time: 103 us; the launch traced here: 102 us
  Pallas kernels  94 us (91%)
  local copies, waits for them, and re-layouts  3.78 us (4%)
  matrix products  2.06 us (2%)
  other arithmetic  1.63 us (2%)
    pallas_call x1, Pallas kernels, flow(): pl.pallas_call(functools.partial(flow_kernel, lax.axis_size('gx'), count_...  29.6 us
    pallas_call x1, Pallas kernels, settle(): pl.pallas_call(functools.partial(settle_kernel, lax.axis_size('gx'), lax....  22.9 us
    pallas_call x1, Pallas kernels, send_back(): pl.pallas_call(functools.partial(return_kernel, count), in_specs=[vmem],...  17.3 us
    pallas_call x1, Pallas kernels, body(): pl.pallas_call(spread_kernel, grid=(steps,), in_specs=[pl.BlockSpec(memor...  15 us
    pallas_call x1, Pallas kernels, body(): pl.pallas_call(sample_kernel, grid=(steps,), in_specs=[pl.BlockSpec(memor...  9.14 us
    unnamed x5, local copies, waits for them, and re-layouts  2.64 us

profile of v6, /device:TPU:1, one launch (start us, length us, event | category | flops | bytes accessed | tf_op | source)
XLA Modules:
  0.0 102.3 jit_solution(18214570618209802400)
XLA Ops:
  0.6 0.0 copy-start
  0.6 0.9 slice_reduce_fusion
  1.6 0.2 select_reduce_fusion
  1.8 0.8 slice_subtract_fusion.1
  2.6 1.2 %fusion = f32[64,1152]{1,0:T(8,128)S(1)} fusion(s32[32]{0:T(128)S(1)} %multiply_add_fusion.12, f32[32,3,128]{2,0,1:T(8,128)} %param.9, f32[32,3,128]{2,0,1:T(8,128)} %param.8, f32[32,3,128]{2,0,1:T(8,128)S(1)} %add_convert_fusion), kind=kOutput, calls=%fused_computation.3 | convolution fusion | flops 28387328 | bytes 442496 | tf_op jit(solution)/shard_map/dot_general | solution.py:454
  3.8 0.1 reshape.130.sent
  3.9 1.0 %copy.44 = f32[32,16,128]{2,0,1:T(8,128)S(1)} copy(f32[32,16,128]{2,1,0:T(8,128)} %param.6) | data formatting | bytes 524288 | tf_op args[1]
  5.0 0.0 copy-done
  5.0 0.3 copy.26
  5.2 0.1 maximum_bitcast_fusion.stacked
  5.3 29.6 %flow.1 = (f32[3,16,32,128]{3,2,1,0:T(8,128)S(1)}, f32[32,18,128]{2,1,0:T(8,128)S(1)}) custom-call(f32[4,16,32,128]{3,2,1,0:T(8,128)S(1)} %maximum_bitcast_fusion.stacked, f32[32,18,128]{2,1,0:T(8,128)S(1)} %reshape.130.sent), custom_call_target="tpu_custom_call" | custom-call | flops 10000000 | bytes 40000000 | tf_op jit(solution)/shard_map/flow/pallas_call | solution.py:369
  35.0 0.1 copy.43
  35.7 15.0 %spread.1 = (f32[3,640,128]{2,1,0:T(8,128)S(1)}, f32[3,5,8,128]{3,2,1,0:T(8,128)S(1)}, f32[3,5,8,128]{3,2,1,0:T(8,128)S(1)}, bf16[8,144,1024]{2,1,0:T(8,128)(2,1...) custom-call(s32[3,8,8,128]{3,2,1,0:T(8,128)S(1)} %get-tuple-element.33.cells, ...), custom_call_target="tpu_custom_call" | custom-call | tf_op jit(solution)/shard_map/spread/pallas_call | solution.py:468
  50.7 22.9 %settle.1 = (f32[3,16,32,128]{3,2,1,0:T(8,128)S(1)}, bf16[3,20,32,256]{3,2,1,0:T(8,128)(2,1)S(1)}) custom-call(f32[3,16,32,128]{3,2,1,0:T(8,128)S(1)} %get-tuple-element.12.second, f32[3,20,32,128]{3,2,1,0:T(8,128)S(1)} %bitcast.82, f32[3,5,8,128]{3,2,1,0:T(8,128)S(1)} %get-tuple-element.15.above, f32[3,5,8,128]{3,2,1,0:T(8,128)S(1)} %get-tuple-element.16.below), custom_call_target="tpu_custom_call" | custom-call | tf_op jit(solution)/shard_map/settle/pallas_call | solution.py:401
  73.6 1.3 %copy.30 = f32[3,32,16,128]{3,2,1,0:T(8,128)} copy(f32[3,32,16,128]{3,1,2,0:T(8,128)S(1)} %bitcast.83) | data formatting | bytes 1572864
  75.0 9.1 %sample.1.source = f32[32,6,128]{2,1,0:T(8,128)S(1)} custom-call(bf16[3,640,256]{2,1,0:T(8,128)(2,1)S(1)} %bitcast.81, bf16[8,144,1024]{2,1,0:T(8,128)(2,1)S(1)} %get-tuple-element.19.y_ref, f32[8,24,1024]{2,1,0:T(8,128)S(1)} %get-tuple-element.20.x_ref, f32[8,32,1024]{2,1,0:T(8,128)S(1)} %get-tuple-element.21.z_ref), custom_call_target="tpu_custom_call" | custom-call | tf_op jit(solution)/shard_map/sample/pallas_call | solution.py:507
  84.1 17.3 %send_back.1 = f32[32,6,128]{2,1,0:T(8,128)S(1)} custom-call(f32[32,6,128]{2,1,0:T(8,128)S(1)} %sample.1.source), custom_call_target="tpu_custom_call" | custom-call | tf_op jit(solution)/shard_map/send_back/pallas_call | solution.py:187
  101.4 0.8 fusion.3
  (18 shorter events, 0.6 us)
Async XLA Ops:
  0.6 4.3 %copy-start = (f32[3,32,16,128]{3,2,1,0:T(8,128)S(1)}, f32[3,32,16,128]{3,2,1,0:T(8,128)}, u32[]{:S(2)}) copy-start(f32[3,32,16,128]{3,2,1,0:T(8,128)} %param.5) | copy-start | bytes 2359300
